TPU v7x, 512 devices: a whole 4x4x16 slice. The times are simulated.
512 devices in a mesh: dp: 32 (over z, core), expert: 16 (over y, x).
Axes of the slice: x: 4, y: 4, z: 16, core: 2. Of those that a mesh axis runs over, the one named last changes fastest.
Arguments:
- feats: bfloat16 [65536, 1152], P(('dp', 'expert')), may hold values from -6 to 6
- proj: bfloat16 [1152, 1024], replicated, may hold values from -0.1875 to 0.1875
- proj_bias: float32 [1024], replicated, may hold values from -3 to 3
- norm_gain: float32 [1024], replicated, may hold values from 0.1 to 1.9
- expert_ids: int32 [65536, 6], P(('dp', 'expert')), may hold values from 0 to 31, all different within a row; in each aligned block of 128 rows (0 to 127, 128 to 255, ...) at most 25 rows name the same one
- gate_codes: int32 [65536, 6], P(('dp', 'expert')), may hold values from 4 to 64
- w_gate: bfloat16 [32, 1024, 768], P('expert', 'dp'), may hold values from -0.1875 to 0.1875
- w_up: bfloat16 [32, 1024, 768], P('expert', 'dp'), may hold values from -0.1875 to 0.1875
- w_down_t: bfloat16 [32, 1024, 768], P('expert', 'dp'), may hold values from -0.21875 to 0.21875
- out_grad: bfloat16 [65536, 1024], P(('dp', 'expert')), may hold values from -6 to 6
Outputs:
- layer_out: bfloat16 [65536, 1024], P(('dp', 'expert'))
- feat_grad: bfloat16 [65536, 1152], P(('dp', 'expert'))
Inputs may be any that keep to these rules, and one draw needn't show every extreme that they name: `expert_ids`: each row names 6 different experts. Among the 128 rows of one device no expert is named by more than 25 rows, and in some device's rows one expert is named by exactly 25.
All inputs are finite; a program needn't handle non-finite values.
Results may differ from a plain program's by a relative error of at most 0.017.
Values may be sent and summed in bfloat16 or wider, within the bound.
No kernel may reach another device: no remote copies, remote signals or barrier semaphores. Data moves between devices by JAX's collectives and lax.ppermute only.
A program may use at most 64 MiB of HBM per device.

v0:
```python
import jax
import jax.numpy as jnp
from jax import lax
from jax.sharding import PartitionSpec as P

CAP = 25


epsilon = 1e-06


def silu_parts(pre_gate):
    sigmoid = jax.nn.sigmoid(pre_gate)
    return (pre_gate * sigmoid, sigmoid * (1.0 + pre_gate * (1.0 - sigmoid)))


def expert_forward(slot_rows, w_gate, w_up, w_down_t):
    full_gate, full_up, full_down = (
        lax.all_gather(w_gate, "dp", axis=1, tiled=True),
        lax.all_gather(w_up, "dp", axis=1, tiled=True),
        lax.all_gather(w_down_t, "dp", axis=1, tiled=True),
    )
    pre_gate = jnp.einsum("lrd,ldf->lrf", slot_rows, full_gate, preferred_element_type=jnp.float32)
    pre_up = jnp.einsum("lrd,ldf->lrf", slot_rows, full_up, preferred_element_type=jnp.float32)
    swished, slopes = silu_parts(pre_gate)
    mixed = (swished * pre_up).astype(jnp.bfloat16)
    expert_out = jnp.einsum("lrf,ldf->lrd", mixed, full_down, preferred_element_type=jnp.float32)
    return (expert_out.astype(jnp.bfloat16), (pre_gate, pre_up, full_gate, full_up, full_down))


def expert_backward(slot_grads, saved):
    pre_gate, pre_up, full_gate, full_up, full_down = saved
    swished, slopes = silu_parts(pre_gate)
    grad_hidden = jnp.einsum(
        "lrd,ldf->lrf", slot_grads, full_down, preferred_element_type=jnp.float32
    )
    grad_gate = (grad_hidden * pre_up * slopes).astype(jnp.bfloat16)
    grad_up = (grad_hidden * swished).astype(jnp.bfloat16)
    expert_grad = jnp.einsum(
        "lrf,ldf->lrd", grad_gate, full_gate, preferred_element_type=jnp.float32
    ) + jnp.einsum("lrf,ldf->lrd", grad_up, full_up, preferred_element_type=jnp.float32)
    return expert_grad.astype(jnp.bfloat16)


def shards(
    feats, proj, proj_bias, norm_gain, expert_ids, gate_codes, w_gate, w_up, w_down_t, out_grad
):
    hidden_in = (jnp.dot(feats, proj, preferred_element_type=jnp.float32) + proj_bias).astype(
        jnp.bfloat16
    )
    hidden_f = hidden_in.astype(jnp.float32)
    inv_rms = lax.rsqrt(jnp.mean(hidden_f * hidden_f, axis=1, keepdims=True) + epsilon)
    normed = (hidden_f * inv_rms * norm_gain).astype(jnp.bfloat16)
    sources = lax.axis_size("expert")
    local_count = w_gate.shape[0]
    expert_total = local_count * sources
    token_count, pick_count = expert_ids.shape
    model_width = hidden_in.shape[1]
    flat_ids = expert_ids.reshape(-1)
    onehot = (flat_ids[:, None] == jnp.arange(expert_total, dtype=jnp.int32)).astype(jnp.int32)
    before = jnp.cumsum(onehot, axis=0) - onehot
    slot_index = jnp.sum(before * onehot, axis=1)
    target = flat_ids * CAP + slot_index
    token_id = jnp.arange(token_count * pick_count, dtype=jnp.int32) // pick_count
    slot_token = jnp.zeros((expert_total * CAP,), jnp.int32).at[target].set(token_id)
    gate_values = gate_codes.astype(jnp.float32) / 64.0
    flat_shape = (expert_total, CAP, model_width)
    send_rows = normed[slot_token].reshape(flat_shape)
    grad_rows = out_grad[slot_token].reshape(flat_shape)
    recv_rows = lax.all_to_all(send_rows, "expert", split_axis=0, concat_axis=1, tiled=True)
    expert_out, saved = expert_forward(recv_rows, w_gate, w_up, w_down_t)
    back_out = lax.all_to_all(expert_out, "expert", split_axis=1, concat_axis=0, tiled=True)
    recv_grads = lax.all_to_all(grad_rows, "expert", split_axis=0, concat_axis=1, tiled=True)
    expert_grad = expert_backward(recv_grads, saved)
    back_grad = lax.all_to_all(expert_grad, "expert", split_axis=1, concat_axis=0, tiled=True)
    picked_out = back_out.reshape(expert_total * CAP, model_width)[target].reshape(
        token_count, pick_count, model_width
    )
    routed = jnp.sum(gate_values[:, :, None] * picked_out.astype(jnp.float32), axis=1)
    layer_out = (hidden_f + routed).astype(jnp.bfloat16)
    picked_grad = back_grad.reshape(expert_total * CAP, model_width)[target].reshape(
        token_count, pick_count, model_width
    )
    routed_grad = jnp.sum(gate_values[:, :, None] * picked_grad.astype(jnp.float32), axis=1)
    scaled = routed_grad * norm_gain
    centre = jnp.mean(hidden_f * scaled, axis=1, keepdims=True)
    input_grad = (
        out_grad.astype(jnp.float32) + inv_rms * scaled - hidden_f * inv_rms**3 * centre
    ).astype(jnp.bfloat16)
    feat_grad = jnp.dot(input_grad, proj.T, preferred_element_type=jnp.float32).astype(jnp.bfloat16)
    return (layer_out, feat_grad)


def solution(mesh):
    in_specs = (
        P(("dp", "expert"), None),
        P(),
        P(),
        P(),
        P(("dp", "expert"), None),
        P(("dp", "expert"), None),
        P("expert", "dp", None),
        P("expert", "dp", None),
        P("expert", "dp", None),
        P(("dp", "expert"), None),
    )
    out_specs = (P(("dp", "expert"), None), P(("dp", "expert"), None))
    return jax.shard_map(shards, mesh=mesh, in_specs=in_specs, out_specs=out_specs, check_vma=False)
```

profile of v0, /device:TPU:1, one launch (start us, length us, event | category | flops | bytes accessed | tf_op | source)
XLA Modules:
  0.0 344.8 jit_solution(7536051152362460647)
XLA Ops:
  13.6 3.4 scatter_custom_fusion
  18.8 4.1 %gather_fusion = bf16[800,1024]{1,0:T(8,128)(2,1)} fusion(bf16[128,1024]{1,0:T(8,128)(2,1)S(1)} %multiply_convert_fusion.6, s32[1024]{0:T(1024)S(1)} %pad_clamp_fusion.1), kind=kCustom, calls=%fused_computation | custom fusion | bytes 3280000 | tf_op jit(solution)/shard_map/gather | solution.py:68
  22.9 2.8 reshape.92
  25.7 7.8 %all-to-all-start = ((bf16[32,25,1024]{2,1,0:T(8,128)(2,1)}), bf16[32,25,1024]{2,1,0:T(8,128)(2,1)}, u32[]{:S(2)}, u32[]{:S(2)}) async-start(bf16[32,25,1024]{2,1,0:T(8,128)(2,1)} %reshape.92), calls=%async_computation | async-start | bytes 4194304 | tf_op jit(solution)/shard_map/all_to_all | solution.py:70
  33.5 4.1 %gather_fusion.2 = bf16[800,1024]{1,0:T(8,128)(2,1)} fusion(bf16[128,1024]{1,0:T(8,128)(2,1)S(1)} %copy-done.1, s32[1024]{0:T(1024)S(1)} %pad_clamp_fusion.1), kind=kCustom, calls=%fused_computation.2 | custom fusion | bytes 3280000 | tf_op jit(solution)/shard_map/gather | solution.py:69
  37.6 2.7 reshape.94
  40.3 18.0 %all-to-all-done = bf16[32,25,1024]{2,1,0:T(8,128)(2,1)} async-done(((bf16[32,25,1024]{2,1,0:T(8,128)(2,1)}), bf16[32,25,1024]{2,1,0:T(8,128)(2,1)}, u32[]{:S(2)}, u32[]{:S(2)}) %all-to-all-start) | async-done | bytes 1638432 | tf_op jit(solution)/shard_map/all_to_all | solution.py:70
  58.3 7.5 %all-to-all-start.2 = ((bf16[32,25,1024]{2,1,0:T(8,128)(2,1)}), bf16[32,25,1024]{2,1,0:T(8,128)(2,1)}, u32[]{:S(2)}, u32[]{:S(2)}) async-start(bf16[32,25,1024]{2,1,0:T(8,128)(2,1)} %reshape.94), calls=%async_computation.2 | async-start | bytes 4194304 | tf_op jit(solution)/shard_map/all_to_all | solution.py:73
  65.9 4.5 %copy.48 = bf16[16,2,25,1024]{3,1,2,0:T(2,128)(2,1)} copy(bf16[16,2,25,1024]{3,2,1,0:T(8,128)(2,1)} %bitcast.1) | data formatting | bytes 3276800 | tf_op jit(solution)/shard_map/all_to_all | solution.py:70
  70.4 20.7 %all-to-all-done.2 = bf16[32,25,1024]{2,1,0:T(8,128)(2,1)} async-done(((bf16[32,25,1024]{2,1,0:T(8,128)(2,1)}), bf16[32,25,1024]{2,1,0:T(8,128)(2,1)}, u32[]{:S(2)}, u32[]{:S(2)}) %all-to-all-start.2) | async-done | bytes 1638432 | tf_op jit(solution)/shard_map/all_to_all | solution.py:73
  91.1 4.5 %copy.50 = bf16[16,2,25,1024]{3,1,2,0:T(2,128)(2,1)} copy(bf16[16,2,25,1024]{3,2,1,0:T(8,128)(2,1)} %bitcast.8) | data formatting | bytes 3276800 | tf_op jit(solution)/shard_map/all_to_all | solution.py:73
  95.6 5.2 %fusion.5 = f32[2,400,768]{2,1,0:T(8,128)} fusion(bf16[2,1024,768]{2,1,0:T(8,128)(2,1)} %all-gather.4.cloned.1.call-done, bf16[2,400,1024]{2,0,1:T(2,128)(2,1)} %bitcast.46), kind=kOutput, calls=%fused_computation.19 | convolution fusion | flops 1258291200 | bytes 7241728 | tf_op jit(solution)/shard_map/lrd,ldf->lrf/dot_general | solution.py:23
  100.8 59.7 %all-gather.6.cloned.1.call-done = bf16[2,1024,768]{2,1,0:T(8,128)(2,1)} async-done(((bf16[2,32,768]{2,1,0:T(8,128)(2,1)}), bf16[2,1024,768]{2,1,0:T(8,128)(2,1)}) %all-gather.6.cloned.1.call-update) | async-done | bytes 3145744 | tf_op jit(solution)/shard_map/all_gather | solution.py:20
  160.5 5.3 %fusion.3 = f32[2,400,768]{2,1,0:T(8,128)} fusion(bf16[2,1024,768]{2,1,0:T(8,128)(2,1)} %all-gather.6.cloned.1.call-done, bf16[2,400,1024]{2,0,1:T(2,128)(2,1)} %bitcast.47), kind=kOutput, calls=%fused_computation.17 | convolution fusion | flops 1258291200 | bytes 7241728 | tf_op jit(solution)/shard_map/lrd,ldf->lrf/dot_general | solution.py:24
  165.8 66.6 %all-gather.8.cloned.1.call-done = bf16[2,1024,768]{2,1,0:T(8,128)(2,1)} async-done(((bf16[2,32,768]{2,1,0:T(8,128)(2,1)}), bf16[2,1024,768]{2,1,0:T(8,128)(2,1)}) %all-gather.8.cloned.1.call-update) | async-done | bytes 3145744 | tf_op jit(solution)/shard_map/all_gather | solution.py:21
  232.4 4.0 %fusion.1 = f32[2,400,768]{2,1,0:T(8,128)S(1)} fusion(bf16[2,1024,768]{2,1,0:T(8,128)(2,1)} %all-gather.8.cloned.1.call-done, bf16[2,400,1024]{2,0,1:T(2,128)(2,1)} %bitcast.48), kind=kOutput, calls=%fused_computation.15 | convolution fusion | flops 1258291200 | bytes 7241728 | tf_op jit(solution)/shard_map/lrd,ldf->lrf/dot_general | solution.py:34
  240.6 2.9 copy.45
  243.5 6.8 %all-to-all-start.3 = ((bf16[2,400,1024]{2,0,1:T(2,128)(2,1)}), bf16[2,400,1024]{2,0,1:T(2,128)(2,1)}, u32[]{:S(2)}, u32[]{:S(2)}) async-start(bf16[2,400,1024]{2,0,1:T(2,128)(2,1)} %copy.45), calls=%async_computation.3 | async-start | bytes 3276800 | tf_op jit(solution)/shard_map/all_to_all | solution.py:75
  250.3 4.8 %convolution_convert_fusion.1 = bf16[2,400,1024]{2,1,0:T(8,128)(2,1)S(1)} fusion(bf16[2,1024,768]{2,1,0:T(8,128)(2,1)} %all-gather.8.cloned.1.call-done, f32[2,400,768]{2,1,0:T(8,128)} %fusion.3, f32[2,400,768]{2,1,0:T(8,128)} %fusion.5), kind=kOutput, calls=%fused_computation.14 | convolution fusion | flops 1262796800 | bytes 9699328 | tf_op jit(solution)/shard_map/lrf,ldf->lrd/dot_general | solution.py:27
  255.1 2.9 copy.40
  258.0 17.8 %all-to-all-done.3 = bf16[2,400,1024]{2,0,1:T(2,128)(2,1)} async-done(((bf16[2,400,1024]{2,0,1:T(2,128)(2,1)}), bf16[2,400,1024]{2,0,1:T(2,128)(2,1)}, u32[]{:S(2)}, u32[]{:S(2)}) %all-to-all-start.3) | async-done | bytes 1638432 | tf_op jit(solution)/shard_map/all_to_all | solution.py:75
  275.8 4.4 %all-to-all-start.1 = ((bf16[2,400,1024]{2,0,1:T(2,128)(2,1)}), bf16[2,400,1024]{2,0,1:T(2,128)(2,1)}, u32[]{:S(2)}, u32[]{:S(2)}) async-start(bf16[2,400,1024]{2,0,1:T(2,128)(2,1)} %copy.40), calls=%async_computation.1 | async-start | bytes 3276800 | tf_op jit(solution)/shard_map/all_to_all | solution.py:72
  280.3 3.4 copy.46
  283.7 2.7 reshape.95
  286.5 16.4 %all-to-all-done.1 = bf16[2,400,1024]{2,0,1:T(2,128)(2,1)} async-done(((bf16[2,400,1024]{2,0,1:T(2,128)(2,1)}), bf16[2,400,1024]{2,0,1:T(2,128)(2,1)}, u32[]{:S(2)}, u32[]{:S(2)}) %all-to-all-start.1) | async-done | bytes 1638432 | tf_op jit(solution)/shard_map/all_to_all | solution.py:72
  302.9 3.4 copy.41
  306.3 2.7 reshape.93
  309.0 6.2 %gather_fusion.3 = bf16[768,1024]{1,0:T(8,128)(2,1)} fusion(bf16[800,1024]{1,0:T(8,128)(2,1)} %reshape.95, s32[1024]{0:T(1024)S(1)} %pad_clamp_fusion), kind=kCustom, calls=%fused_computation.3 | custom fusion | bytes 3148800 | tf_op jit(solution)/shard_map/gather | solution.py:81
  315.2 6.2 %gather_fusion.1 = bf16[768,1024]{1,0:T(8,128)(2,1)} fusion(bf16[800,1024]{1,0:T(8,128)(2,1)} %reshape.93, s32[1024]{0:T(1024)S(1)} %pad_clamp_fusion), kind=kCustom, calls=%fused_computation.1 | custom fusion | bytes 3148800 | tf_op jit(solution)/shard_map/gather | solution.py:76
  321.4 3.9 %reshape.96 = f32[128,6,1024]{2,1,0:T(8,128)} reshape(bf16[768,1024]{1,0:T(8,128)(2,1)} %gather_fusion.1) | data formatting | bytes 4718592 | tf_op jit(solution)/shard_map/convert_element_type | solution.py:79
  325.3 3.9 %reshape.97 = f32[128,6,1024]{2,1,0:T(8,128)} reshape(bf16[768,1024]{1,0:T(8,128)(2,1)} %gather_fusion.3) | data formatting | bytes 4718592 | tf_op jit(solution)/shard_map/convert_element_type | solution.py:84
  329.3 6.6 %multiply_reduce_fusion = (f32[128,1024]{1,0:T(8,128)S(1)}, f32[128,1024]{1,0:T(8,128)S(1)}) fusion(f32[128,6,1024]{2,1,0:T(8,128)} %reshape.97, f32[128,6]{1,0:T(8,128)S(1)} %copy.31, f32[128,6,1024]{2,1,0:T(8,128)} %reshape.96), kind=kLoop, calls=%fused_computation.5 | loop fusion | flops 2883584 | bytes 7343104 | tf_op jit(solution)/shard_map/reduce_sum | solution.py:84
  (49 shorter events, 14.8 us)
Async XLA Ops:
  7.2 9.9 %copy-start = (bf16[1152,1024]{1,0:T(8,128)(2,1)S(1)}, bf16[1152,1024]{1,0:T(8,128)(2,1)}, u32[]{:S(2)}) copy-start(bf16[1152,1024]{1,0:T(8,128)(2,1)} %param.11) | copy-start | bytes 7077892
  7.2 11.5 %copy-start.2 = (f32[1024]{0:T(1024)S(1)}, f32[1024]{0:T(1024)}, u32[]{:S(2)}) copy-start(f32[1024]{0:T(1024)} %param.13) | copy-start | bytes 12292
  7.2 88.4 %all-gather.4.cloned.1.call-start = ((), (), s32[]{:S(2)}) async-start(), calls=%async_computation.4 | async-start | bytes 3244032 | tf_op jit(solution)/shard_map/all_gather | solution.py:19
  7.9 152.6 %all-gather.6.cloned.1.call-start = ((), (), s32[]{:S(2)}) async-start(), calls=%async_computation.5 | async-start | bytes 3244032 | tf_op jit(solution)/shard_map/all_gather | solution.py:20
  8.7 223.7 %all-gather.8.cloned.1.call-start = ((), (), s32[]{:S(2)}) async-start(), calls=%async_computation.6 | async-start | bytes 3244032 | tf_op jit(solution)/shard_map/all_gather | solution.py:21
  25.7 7.8 %copy-start.1 = (bf16[128,1024]{1,0:T(8,128)(2,1)S(1)}, bf16[128,1024]{1,0:T(8,128)(2,1)}, u32[]{:S(2)}) copy-start(bf16[128,1024]{1,0:T(8,128)(2,1)} %param.19) | copy-start | bytes 786436
  25.7 32.6 %all-to-all-start = ((bf16[32,25,1024]{2,1,0:T(8,128)(2,1)}), bf16[32,25,1024]{2,1,0:T(8,128)(2,1)}, u32[]{:S(2)}, u32[]{:S(2)}) async-start(bf16[32,25,1024]{2,1,0:T(8,128)(2,1)} %reshape.92), calls=%async_computation | async-start | bytes 4194304 | tf_op jit(solution)/shard_map/all_to_all | solution.py:70
  58.3 32.8 %all-to-all-start.2 = ((bf16[32,25,1024]{2,1,0:T(8,128)(2,1)}), bf16[32,25,1024]{2,1,0:T(8,128)(2,1)}, u32[]{:S(2)}, u32[]{:S(2)}) async-start(bf16[32,25,1024]{2,1,0:T(8,128)(2,1)} %reshape.94), calls=%async_computation.2 | async-start | bytes 4194304 | tf_op jit(solution)/shard_map/all_to_all | solution.py:73
  232.4 4.0 %copy-start.4 = (bf16[2,1024,768]{2,1,0:T(8,128)(2,1)S(1)}, bf16[2,1024,768]{2,1,0:T(8,128)(2,1)}, u32[]{:S(2)}) copy-start(bf16[2,1024,768]{2,1,0:T(8,128)(2,1)} %all-gather.4.cloned.1.call-done) | copy-start | bytes 9437188
  232.4 4.1 %copy-start.6 = (f32[2,400,768]{2,1,0:T(8,128)S(1)}, f32[2,400,768]{2,1,0:T(8,128)}, u32[]{:S(2)}) copy-start(f32[2,400,768]{2,1,0:T(8,128)} %fusion.5) | copy-start | bytes 7372804
  232.4 4.8 %copy-start.7 = (f32[2,400,768]{2,1,0:T(8,128)S(1)}, f32[2,400,768]{2,1,0:T(8,128)}, u32[]{:S(2)}) copy-start(f32[2,400,768]{2,1,0:T(8,128)} %fusion.3) | copy-start | bytes 7372804
  237.2 1.9 copy-start.5
  243.5 32.3 %all-to-all-start.3 = ((bf16[2,400,1024]{2,0,1:T(2,128)(2,1)}), bf16[2,400,1024]{2,0,1:T(2,128)(2,1)}, u32[]{:S(2)}, u32[]{:S(2)}) async-start(bf16[2,400,1024]{2,0,1:T(2,128)(2,1)} %copy.45), calls=%async_computation.3 | async-start | bytes 3276800 | tf_op jit(solution)/shard_map/all_to_all | solution.py:75
  255.1 25.1 %copy-start.3 = (s32[128,6]{0,1:T(8,128)S(1)}, s32[128,6]{0,1:T(8,128)}, u32[]{:S(2)}) copy-start(s32[128,6]{0,1:T(8,128)} %param.15) | copy-start | bytes 9220
  275.8 27.1 %all-to-all-start.1 = ((bf16[2,400,1024]{2,0,1:T(2,128)(2,1)}), bf16[2,400,1024]{2,0,1:T(2,128)(2,1)}, u32[]{:S(2)}, u32[]{:S(2)}) async-start(bf16[2,400,1024]{2,0,1:T(2,128)(2,1)} %copy.40), calls=%async_computation.1 | async-start | bytes 3276800 | tf_op jit(solution)/shard_map/all_to_all | solution.py:72
Sparse Core Ops, SparseCore 0:
  10.1 78.4 all-gather.3
  90.8 69.6 all-gather.5
  162.6 69.7 all-gather.7
where the time goes:
time: 347 us; the launch traced here: 345 us
  waiting for transfers between devices  201 us (58%)
  local copies, waits for them, and re-layouts  67.2 us (19%)
  starting transfers between devices  26.6 us (8%)
  matrix products  25.7 us (7%)
  between operations  14 us (4%)
  other arithmetic  10.1 us (3%)
    all_gather x1, waiting for transfers between devices, expert_forward(): lax.all_gather(w_down_t, 'dp', axis=1, tiled=True)  66.6 us
    all_gather x1, waiting for transfers between devices, expert_forward(): lax.all_gather(w_up, 'dp', axis=1, tiled=True)  59.7 us
    all_to_all x1, waiting for transfers between devices, shards(): lax.all_to_all(grad_rows, 'expert', split_axis=0, concat_axis=1, tiled=True)  20.7 us
    all_to_all x1, waiting for transfers between devices, shards(): lax.all_to_all(send_rows, 'expert', split_axis=0, concat_axis=1, tiled=True)  18 us
    all_to_all x1, waiting for transfers between devices, shards(): lax.all_to_all(expert_grad, 'expert', split_axis=1, concat_axis=0, tiled=...  17.8 us
    all_to_all x1, waiting for transfers between devices, shards(): lax.all_to_all(expert_out, 'expert', split_axis=1, concat_axis=0, tiled=T...  16.4 us
    all_to_all x1, starting transfers between devices, shards(): lax.all_to_all(send_rows, 'expert', split_axis=0, concat_axis=1, tiled=True)  7.75 us
    all_to_all x1, starting transfers between devices, shards(): lax.all_to_all(grad_rows, 'expert', split_axis=0, concat_axis=1, tiled=True)  7.53 us
  transfers between devices with their start and end apart: 7, of which 6 were waited for; matrix products, arithmetic and copies ran while one was open for 16% of the time, Pallas kernels for 0%

commit v1 on v0

v1 whole, which is shorter than its diff:
```python
import jax
import jax.numpy as jnp
from jax import lax
from jax.experimental import pallas as pl
from jax.experimental.pallas import tpu as pltpu
from jax.sharding import PartitionSpec as P

CAP = 25
HALF = 56
SEND = 2 * HALF
WIN = 32
BACK = 104
SHIFT = 2
EPS = 1e-06
NO_SLOT = 200.0
BF = jnp.bfloat16
F32 = jnp.float32


def mm(a, b):
    return lax.dot_general(a, b, (((1,), (0,)), ((), ())), preferred_element_type=F32)


def mm_t(a, b):
    return lax.dot_general(a, b, (((1,), (1,)), ((), ())), preferred_element_type=F32)


def slot_rows(rows, offset, n_exp, slot):
    r = lax.broadcasted_iota(jnp.int32, (rows, 1), 0)
    chunk = (r * 1171) >> 16
    m = r - chunk * HALF - offset
    second = (m >= CAP).astype(jnp.int32)
    inside = (m >= 0) & (m < 2 * CAP)
    slot_of = jnp.where(inside, m - CAP * second, 99).astype(F32)
    lane = lax.broadcasted_iota(jnp.int32, (rows, n_exp), 1)
    pick = jnp.where(lane == 2 * chunk + second, 1.0, 0.0).astype(BF)
    return pick, mm(pick, slot) == slot_of


def prepare_kernel(
    feats, proj, bias, gain, ids, codes, grads, send, hidden, inv, mix_out, mix_grad
):
    sources = send.shape[0]
    rows = sources * HALF
    toks, width = grads.shape
    n_exp = 2 * sources
    lane = lax.broadcasted_iota(jnp.int32, (n_exp, toks), 0)
    member = jnp.zeros((n_exp, toks), F32)
    weight = jnp.zeros((n_exp, toks), F32)
    for k in range(ids.shape[0]):
        hit = lane == ids[k : k + 1, :]
        member = member + jnp.where(hit, 1.0, 0.0)
        weight = weight + jnp.where(hit, codes[k : k + 1, :].astype(F32) / 64.0, 0.0)
    weight = weight.astype(BF)
    earlier = lax.broadcasted_iota(jnp.int32, (toks, toks), 0) < lax.broadcasted_iota(
        jnp.int32, (toks, toks), 1
    )
    before = mm(member.astype(BF), jnp.where(earlier, 1.0, 0.0).astype(BF))
    slot = jnp.where(member > 0.5, before, NO_SLOT).astype(BF)
    pick, chosen = slot_rows(rows, 0, n_exp, slot)
    select = jnp.where(chosen, 1.0, 0.0).astype(BF)
    send[:, HALF:SEND, :] = mm(select, grads[...]).astype(BF).reshape(sources, HALF, width)
    h = (mm(feats[...], proj[...]) + bias[...]).astype(BF)
    hidden[...] = h
    hf = h.astype(F32)
    scale = lax.rsqrt(jnp.mean(hf * hf, axis=1, keepdims=True) + EPS)
    inv[...] = scale
    normed = (hf * scale * gain[...]).astype(BF)
    send[:, 0:HALF, :] = mm(select, normed).astype(BF).reshape(sources, HALF, width)
    mix_out[...] = jnp.where(chosen, mm(pick, weight), 0.0).T.astype(BF)
    pick, chosen = slot_rows(rows, SHIFT, n_exp, slot)
    mix_grad[...] = jnp.where(chosen, mm(pick, weight), 0.0).T.astype(BF)


def window(ref, start):
    part = ref[:, start : start + WIN, :]
    return part.reshape(part.shape[0] * WIN, part.shape[2])


def place(ref, outs, grads):
    n = ref.shape[0]
    width = ref.shape[2]
    first, second = (x.reshape(n, WIN, width) for x in outs)
    third, fourth = (pltpu.roll(x, SHIFT, 0).reshape(n, WIN, width) for x in grads)
    row = lax.broadcasted_iota(jnp.int32, (1, 8, 1), 1)

    def seam(count, a, b):
        return jnp.where(row < count, a[:, 24:32, :], b[:, 0:8, :]).astype(BF)

    ref[:, 0:24, :] = first[:, 0:24, :].astype(BF)
    ref[:, 24:32, :] = seam(1, first, second)
    ref[:, 32:48, :] = second[:, 8:24, :].astype(BF)
    ref[:, 48:56, :] = seam(2, second, third)
    ref[:, 56:72, :] = third[:, 8:24, :].astype(BF)
    ref[:, 72:80, :] = seam(3, third, fourth)
    ref[:, 80:104, :] = fourth[:, 8:32, :].astype(BF)


def matrix(buf, j):
    return buf[j].reshape(buf.shape[1] * buf.shape[2], buf.shape[3])


def expert_kernel(rows, weights, back, buf, sems):
    copies = {
        j: pltpu.make_async_copy(weights.at[:, j], buf.at[j], sems.at[j])
        for j in (0, 2, 4, 1, 3, 5)
    }
    for c in copies.values():
        c.start()
    outs, grads = [], []
    for e in range(2):
        x = window(rows, 24 * e)
        copies[e].wait()
        h = mm(x, matrix(buf, e))
        copies[2 + e].wait()
        u = mm(x, matrix(buf, 2 + e))
        sig = jax.nn.sigmoid(h)
        swished = h * sig
        upslope = u * (sig * (1.0 + h * (1.0 - sig)))
        copies[4 + e].wait()
        outs.append(mm_t((swished * u).astype(BF), matrix(buf, 4 + e)))
        g = mm(window(rows, HALF + 24 * e), matrix(buf, 4 + e))
        gate = (g * upslope).astype(BF)
        up = (g * swished).astype(BF)
        grads.append(mm_t(gate, matrix(buf, e)) + mm_t(up, matrix(buf, 2 + e)))
    place(back, outs, grads)


def combine_kernel(back, mix_out, mix_grad, hidden, inv, gain, grads, proj, out, feat_grad):
    n, _, width = back.shape
    hf = hidden[...].astype(F32)
    got = back[:, 0:HALF, :].reshape(n * HALF, width)
    out[...] = (hf + mm(mix_out[...], got)).astype(BF)
    got = back[:, BACK - HALF : BACK, :].reshape(n * HALF, width)
    scaled = mm(mix_grad[...], got) * gain[...]
    scale = inv[...]
    centre = jnp.mean(hf * scaled, axis=1, keepdims=True)
    total = grads[...].astype(F32) + scale * scaled - hf * (scale * scale * scale) * centre
    feat_grad[...] = mm_t(total.astype(BF), proj[...]).astype(BF)


def shape(dims, dtype):
    return jax.ShapeDtypeStruct(dims, dtype)


PARAMS = pltpu.CompilerParams(vmem_limit_bytes=56 * 1024 * 1024)
VMEM = pl.BlockSpec(memory_space=pltpu.VMEM)
ANY = pl.BlockSpec(memory_space=pl.ANY)


def shards(
    feats, proj, proj_bias, norm_gain, expert_ids, gate_codes, w_gate, w_up, w_down_t, out_grad
):
    toks, width = out_grad.shape
    sources = lax.axis_size("expert")
    local, part, ff = w_gate.shape
    bias, gain = proj_bias.reshape(1, width), norm_gain.reshape(1, width)
    stacked = jnp.concatenate([w_gate, w_up, w_down_t], axis=0)
    weights = lax.all_gather(stacked, "dp", axis=0, tiled=False)

    send, hidden, inv, mix_out, mix_grad = pl.pallas_call(
        prepare_kernel,
        out_shape=(
            shape((sources, SEND, width), BF),
            shape((toks, width), BF),
            shape((toks, 1), F32),
            shape((toks, sources * HALF), BF),
            shape((toks, sources * HALF), BF),
        ),
        in_specs=[VMEM] * 7,
        out_specs=(VMEM,) * 5,
        compiler_params=PARAMS,
        name="prepare",
    )(feats, proj, bias, gain, expert_ids.T, gate_codes.T, out_grad)
    received = lax.all_to_all(send, "expert", split_axis=0, concat_axis=0, tiled=True)
    results = pl.pallas_call(
        expert_kernel,
        out_shape=shape((sources, BACK, width), BF),
        in_specs=[VMEM, ANY],
        out_specs=VMEM,
        scratch_shapes=[
            pltpu.VMEM((3 * local, weights.shape[0], part, ff), BF),
            pltpu.SemaphoreType.DMA((3 * local,)),
        ],
        compiler_params=PARAMS,
        name="experts",
    )(received, weights)
    back = lax.all_to_all(results, "expert", split_axis=0, concat_axis=0, tiled=True)
    return pl.pallas_call(
        combine_kernel,
        out_shape=(shape((toks, width), BF), shape(feats.shape, BF)),
        in_specs=[VMEM] * 8,
        out_specs=(VMEM,) * 2,
        compiler_params=PARAMS,
        name="combine",
    )(back, mix_out, mix_grad, hidden, inv, gain, out_grad, proj)


def solution(mesh):
    tokens = P(("dp", "expert"), None)
    experts = P("expert", "dp", None)
    in_specs = (tokens, P(), P(), P(), tokens, tokens, experts, experts, experts, tokens)
    return jax.shard_map(
        shards, mesh=mesh, in_specs=in_specs, out_specs=(tokens, tokens), check_vma=False
    )
```

time: 347 us -> 177 us (0.51)
  waiting for transfers between devices: 201 us -> 31.9 us
  blocking collectives: 0 us -> 98 us
  local copies, waits for them, and re-layouts: 67.2 us -> 0 us
  Pallas kernels: 0 us -> 31.3 us
  starting transfers between devices: 26.6 us -> 0.04 us
  matrix products: 25.7 us -> 0 us
  other arithmetic: 10.1 us -> 1.74 us
    all_to_all x0 -> x2, blocking collectives: none -> 98 us  [the longest x1 49.2 us: shards(): lax.all_to_all(send, 'expert', split_axis=0, concat_axis=0, tiled=True)]
    all_gather x3 -> x1, waiting for transfers between devices: 126 us -> 31.9 us  [shards(): weights = lax.all_gather(stacked, 'dp', axis=0, tiled=False)]
    all_to_all x4 -> x0, waiting for transfers between devices: 72.9 us -> none  [the longest x1 20.7 us: shards(): lax.all_to_all(grad_rows, 'expert', split_axis=0, concat_axis=1, tiled=True)]
    pallas_call x0 -> x3, Pallas kernels: none -> 31.3 us  [the longest x1 20 us: shards(): pl.pallas_call(expert_kernel, out_shape=shape((sources, BACK, width), BF)...]
    all_to_all x4 -> x0, starting transfers between devices: 26.5 us -> none  [the longest x1 7.75 us: shards(): lax.all_to_all(send_rows, 'expert', split_axis=0, concat_axis=1, tiled=True)]
    dot_general x8 -> x0, matrix products: 25.7 us -> none  [the longest x1 5.34 us: expert_forward(): jnp.einsum('lrd,ldf->lrf', slot_rows, full_up, preferred_element_type=jnp...]
    gather x4 -> x0, local copies, waits for them, and re-layouts: 20.6 us -> none  [the longest x1 6.21 us: shards(): back_out.reshape(expert_total * CAP, model_width)[target]]
    all_to_all x4 -> x0, local copies, waits for them, and re-layouts: 15.8 us -> none  [the longest x1 4.5 us: shards(): lax.all_to_all(send_rows, 'expert', split_axis=0, concat_axis=1, tiled=True)]
  transfers between devices with their start and end apart: 7 -> 1, of which waited for: 6 -> 1; matrix products, arithmetic and copies ran while one was open for 16% -> 0% of each run, Pallas kernels for 0% -> 3%
where the time goes in v1:
time: 177 us
  blocking collectives  98 us (55%)
  waiting for transfers between devices  31.9 us (18%)
  Pallas kernels  31.3 us (18%)
  between operations  14 us (8%)
    all_to_all x1, blocking collectives, shards(): lax.all_to_all(send, 'expert', split_axis=0, concat_axis=0, tiled=True)  49.2 us
    all_to_all x1, blocking collectives, shards(): lax.all_to_all(results, 'expert', split_axis=0, concat_axis=0, tiled=True)  48.8 us
    all_gather x1, waiting for transfers between devices, shards(): weights = lax.all_gather(stacked, 'dp', axis=0, tiled=False)  31.9 us
    pallas_call x1, Pallas kernels, shards(): pl.pallas_call(expert_kernel, out_shape=shape((sources, BACK, width), BF)...  20 us
    pallas_call x1, Pallas kernels, shards(): pl.pallas_call(prepare_kernel, out_shape=(shape((sources, SEND, width), B...  5.82 us
    pallas_call x1, Pallas kernels, shards(): pl.pallas_call(combine_kernel, out_shape=(shape((toks, width), BF), shape...  5.45 us
  transfers between devices with their start and end apart: 1, of which 1 were waited for; matrix products, arithmetic and copies ran while one was open for 0% of the time, Pallas kernels for 3%

profile of v1, /device:TPU:1, one launch (start us, length us, event | category | flops | bytes accessed | tf_op | source)
XLA Modules:
  0.0 177.0 jit_solution(16905119468669740759)
XLA Ops:
  7.2 0.0 all-gather.3.cloned.1.call-start
  7.2 1.7 pad_maximum_fusion
  8.9 0.0 all-gather.3.cloned.1.call-update
  9.0 5.8 %prepare.1 = (bf16[16,112,1024]{2,1,0:T(8,128)(2,1)}, bf16[128,1024]{1,0:T(8,128)(2,1)}, f32[128,1]{1,0:T(8,128)}, bf16[128,896]{1,0:T(8,128)(2,1)}, bf16[128,896]{1,0:T(8,128)(2,1)}) custom-call(bf16[128,1152]{1,0:T(8,128)(2,1)} %feats.1, bf16[1152,1024]{1,0:T(8,128)(2,1)} %proj.3, f32[1,1024]{1,0:T(1,128)} %bitcast.8, f32[1,1024]{1,0:T(1,128)} %bitcast.6, ...), custom_call_target="tpu_custom_call" | custom-call | tf_op jit(solution)/shard_map/prepare/pallas_call | solution.py:161
  14.8 49.2 %all_to_all.10.rows = bf16[16,112,1024]{2,1,0:T(8,128)(2,1)} all-to-all(bf16[16,112,1024]{2,1,0:T(8,128)(2,1)} %get-tuple-element.7), channel_id=1, replica_groups=mesh['dp'=32,'expert'=16] {'expert'}, dimensions={0} | all-to-all | bytes 7340032 | tf_op jit(solution)/shard_map/all_to_all | solution.py:175
  63.9 31.9 %all-gather.3.cloned.1.call-done = bf16[192,32,768]{2,1,0:T(8,128)(2,1)} async-done(((bf16[6,32,768]{2,1,0:T(8,128)(2,1)}), bf16[192,32,768]{2,1,0:T(8,128)(2,1)}) %all-gather.3.cloned.1.call-update) | async-done | bytes 9437200 | tf_op jit(solution)/shard_map/all_gather | solution.py:159
  95.8 20.0 %experts.1 = bf16[16,104,1024]{2,1,0:T(8,128)(2,1)} custom-call(bf16[16,112,1024]{2,1,0:T(8,128)(2,1)} %all_to_all.10.rows, bf16[32,6,32,768]{3,2,1,0:T(8,128)(2,1)} %bitcast.5), custom_call_target="tpu_custom_call" | custom-call | tf_op jit(solution)/shard_map/experts/pallas_call | solution.py:176
  115.8 48.8 %all_to_all.11.back = bf16[16,104,1024]{2,1,0:T(8,128)(2,1)} all-to-all(bf16[16,104,1024]{2,1,0:T(8,128)(2,1)} %experts.1), channel_id=1, replica_groups=mesh['dp'=32,'expert'=16] {'expert'}, dimensions={0} | all-to-all | bytes 6815744 | tf_op jit(solution)/shard_map/all_to_all | solution.py:188
  164.7 5.5 %combine.1 = (bf16[128,1024]{1,0:T(8,128)(2,1)}, bf16[128,1152]{1,0:T(8,128)(2,1)}) custom-call(bf16[16,104,1024]{2,1,0:T(8,128)(2,1)} %all_to_all.11.back, bf16[128,896]{1,0:T(8,128)(2,1)} %get-tuple-element.8.mix_out, bf16[128,896]{1,0:T(8,128)(2,1)} %get-tuple-element.9.mix_grad, bf16[128,1024]{1,0:T(8,128)(2,1)} %get-tuple-element.10.hidden, ...), custom_call_target="tpu_custom_call" | custom-call | tf_op jit(solution)/shard_map/combine/pallas_call | solution.py:189
Async XLA Ops:
  7.2 88.6 %all-gather.3.cloned.1.call-start = ((), (), s32[]{:S(2)}) async-start(), calls=%async_computation.2 | async-start | bytes 9732096 | tf_op jit(solution)/shard_map/all_gather | solution.py:159
Sparse Core Ops, SparseCore 0:
  10.7 85.0 all-gather.2

commit v2 on v1

v2 whole, which is shorter than its diff:
```python
import jax
import jax.numpy as jnp
from jax import lax
from jax.experimental import pallas as pl
from jax.experimental.pallas import tpu as pltpu
from jax.sharding import PartitionSpec as P

CHUNK = 104
KINDS = 4
MAIN = 24
LAST = KINDS * MAIN
EPS = 1e-06
NO_SLOT = 200.0
BF = jnp.bfloat16
F32 = jnp.float32


def mm(a, b):
    return lax.dot_general(a, b, (((1,), (0,)), ((), ())), preferred_element_type=F32)


def mm_t(a, b):
    return lax.dot_general(a, b, (((1,), (1,)), ((), ())), preferred_element_type=F32)


def prepare_kernel(feats, proj, bias, gain, ids, codes, grads, send, hidden, inv, mix):
    sources, _, width = send.shape
    rows = sources * CHUNK
    toks = grads.shape[0]
    n_exp = 2 * sources
    lane = lax.broadcasted_iota(jnp.int32, (n_exp, toks), 0)
    member = jnp.zeros((n_exp, toks), F32)
    weight = jnp.zeros((n_exp, toks), F32)
    for k in range(ids.shape[0]):
        hit = lane == ids[k : k + 1, :]
        member = member + jnp.where(hit, 1.0, 0.0)
        weight = weight + jnp.where(hit, codes[k : k + 1, :].astype(F32) / 64.0, 0.0)
    earlier = lax.broadcasted_iota(jnp.int32, (toks, toks), 0) < lax.broadcasted_iota(
        jnp.int32, (toks, toks), 1
    )
    before = mm(member.astype(BF), jnp.where(earlier, 1.0, 0.0).astype(BF))
    slot = jnp.where(member > 0.5, before, NO_SLOT).astype(BF)
    r = lax.broadcasted_iota(jnp.int32, (rows, 1), 0)
    chunk = (r * 40330) >> 22
    m = r - chunk * CHUNK
    kind = jnp.where(m < LAST, (m * 2731) >> 16, m - LAST)
    slot_of = jnp.where(m < LAST, m - MAIN * kind, jnp.where(m < LAST + KINDS, MAIN, 99))
    pick = jnp.where(
        lax.broadcasted_iota(jnp.int32, (rows, n_exp), 1) == 2 * chunk + (kind & 1), 1.0, 0.0
    ).astype(BF)
    chosen = jnp.where(mm(pick, slot) == slot_of.astype(F32), 1.0, 0.0)
    of_token = jnp.where(kind < 2, chosen, 0.0)
    of_grad = jnp.where(kind < 2, 0.0, chosen)
    spread = mm(pick, weight.astype(BF))
    mix[0:toks, :] = (spread * of_token).T.astype(BF)
    mix[toks : 2 * toks, :] = (spread * of_grad).T.astype(BF)
    from_grads = mm(of_grad.astype(BF), grads[...])
    h = (mm(feats[...], proj[...]) + bias[...]).astype(BF)
    hidden[...] = h
    hf = h.astype(F32)
    scale = lax.rsqrt(jnp.mean(hf * hf, axis=1, keepdims=True) + EPS)
    inv[...] = scale
    normed = (hf * scale * gain[...]).astype(BF)
    sent = from_grads + mm(of_token.astype(BF), normed)
    send[...] = sent.reshape(sources, CHUNK, width).astype(BF)


def arrange_kernel(received, rows):
    sources, _, width = received.shape
    last = received[:, LAST:CHUNK, :].astype(F32)
    for k in range(KINDS):
        part = received[:, MAIN * k : MAIN * (k + 1), :].astype(F32)
        rows[k, 0 : sources * MAIN, :] = part.reshape(sources * MAIN, width).astype(BF)
        rows[k, sources * MAIN :, :] = last[:, k, :].astype(BF)


def expert_kernel(rows, weights, back, buf, mixed, d_gate, d_up, sems):
    sources, _, width = back.shape
    total = rows.shape[1]
    shards_of, part, ff = buf.shape[1:]
    half = total // 32 * 16
    blocks = (slice(0, half), slice(half, total))
    copies = {
        j: pltpu.make_async_copy(weights.at[:, j], buf.at[j], sems.at[j])
        for j in (0, 2, 4, 1, 3, 5)
    }
    for c in copies.values():
        c.start()
    ready, last = set(), {}

    def matrix(j):
        if j not in ready:
            copies[j].wait()
            ready.add(j)
        return buf[j].reshape(shards_of * part, ff)

    def store(kind, result):
        main = result[0 : sources * MAIN].reshape(sources, MAIN, width)
        back[:, MAIN * kind : MAIN * (kind + 1), :] = main.astype(BF)
        last[kind] = result[sources * MAIN :].reshape(sources, 1, width)

    def first_products(e):
        h = [mm(rows[e, at, :], matrix(e)) for at in blocks]
        u = [mm(rows[e, at, :], matrix(2 + e)) for at in blocks]
        g = [mm(rows[2 + e, at, :], matrix(4 + e)) for at in blocks]
        return h, u, g

    def elementwise(e, i, h, u, g):
        sig = jax.nn.sigmoid(h[i])
        swished = h[i] * sig
        mixed[e, blocks[i], :] = (swished * u[i]).astype(BF)
        d_gate[e, blocks[i], :] = (g[i] * (u[i] * (sig * (1.0 + h[i] * (1.0 - sig))))).astype(BF)
        d_up[e, blocks[i], :] = (g[i] * swished).astype(BF)

    def second_products(e):
        store(e, mm_t(mixed[e], matrix(4 + e)))
        store(2 + e, mm_t(d_gate[e], matrix(e)) + mm_t(d_up[e], matrix(2 + e)))

    for e in range(2):
        products = first_products(e)
        for i in range(2):
            elementwise(e, i, *products)
        second_products(e)
    row = lax.broadcasted_iota(jnp.int32, (1, CHUNK - LAST, 1), 1)
    rest = jnp.zeros((sources, CHUNK - LAST, width), F32)
    for kind in range(KINDS):
        rest = jnp.where(row == kind, last[kind], rest)
    back[:, LAST:CHUNK, :] = rest.astype(BF)


def stack_kernel(w_gate, w_up, w_down_t, out, sems):
    local = w_gate.shape[0]
    copies = [
        pltpu.make_async_copy(w, out.at[i * local : (i + 1) * local], sems.at[i])
        for i, w in enumerate((w_gate, w_up, w_down_t))
    ]
    for c in copies:
        c.start()
    for c in copies:
        c.wait()


def combine_kernel(back, mix, hidden, inv, gain, grads, proj, out, feat_grad):
    n, _, width = back.shape
    toks = hidden.shape[0]
    hf = hidden[...].astype(F32)
    sums = mm(mix[...], back[...].reshape(n * CHUNK, width))
    out[...] = (hf + sums[0:toks]).astype(BF)
    scaled = sums[toks : 2 * toks] * gain[...]
    scale = inv[...]
    centre = jnp.mean(hf * scaled, axis=1, keepdims=True)
    total = grads[...].astype(F32) + scale * scaled - hf * (scale * scale * scale) * centre
    feat_grad[...] = mm_t(total.astype(BF), proj[...]).astype(BF)


def shape(dims, dtype):
    return jax.ShapeDtypeStruct(dims, dtype)


def params(mib):
    return pltpu.CompilerParams(vmem_limit_bytes=mib * 1024 * 1024)


VMEM = pl.BlockSpec(memory_space=pltpu.VMEM)
HBM = pl.BlockSpec(memory_space=pltpu.HBM)


def shards(
    feats, proj, proj_bias, norm_gain, expert_ids, gate_codes, w_gate, w_up, w_down_t, out_grad
):
    toks, width = out_grad.shape
    sources = lax.axis_size("expert")
    local, part, ff = w_gate.shape
    bias, gain = proj_bias.reshape(1, width), norm_gain.reshape(1, width)
    stacked = pl.pallas_call(
        stack_kernel,
        out_shape=shape((3 * local, part, ff), BF),
        in_specs=[HBM] * 3,
        out_specs=HBM,
        scratch_shapes=[pltpu.SemaphoreType.DMA((3,))],
        compiler_params=params(16),
        name="stack",
    )(w_gate, w_up, w_down_t)
    weights = lax.all_gather(stacked, "dp", axis=0, tiled=False)

    send, hidden, inv, mix = pl.pallas_call(
        prepare_kernel,
        out_shape=(
            shape((sources, CHUNK, width), BF),
            shape((toks, width), BF),
            shape((toks, 1), F32),
            shape((2 * toks, sources * CHUNK), BF),
        ),
        in_specs=[VMEM] * 7,
        out_specs=(VMEM,) * 4,
        compiler_params=params(28),
        name="prepare",
    )(feats, proj, bias, gain, expert_ids.T, gate_codes.T, out_grad)
    received = lax.all_to_all(send, "expert", split_axis=0, concat_axis=0, tiled=True)
    slots = sources * (MAIN + 1)
    rows = pl.pallas_call(
        arrange_kernel,
        out_shape=shape((KINDS, slots, width), BF),
        in_specs=[VMEM],
        out_specs=VMEM,
        compiler_params=params(28),
        name="arrange",
    )(received)
    results = pl.pallas_call(
        expert_kernel,
        out_shape=shape((sources, CHUNK, width), BF),
        in_specs=[VMEM, HBM],
        out_specs=VMEM,
        scratch_shapes=[
            pltpu.VMEM((3 * local, weights.shape[0], part, ff), BF),
            pltpu.VMEM((local, slots, ff), BF),
            pltpu.VMEM((local, slots, ff), BF),
            pltpu.VMEM((local, slots, ff), BF),
            pltpu.SemaphoreType.DMA((3 * local,)),
        ],
        compiler_params=params(46),
        name="experts",
    )(rows, weights)
    back = lax.all_to_all(results, "expert", split_axis=0, concat_axis=0, tiled=True)
    return pl.pallas_call(
        combine_kernel,
        out_shape=(shape((toks, width), BF), shape(feats.shape, BF)),
        in_specs=[VMEM] * 7,
        out_specs=(VMEM,) * 2,
        compiler_params=params(28),
        name="combine",
    )(back, mix, hidden, inv, gain, out_grad, proj)


def solution(mesh):
    tokens = P(("dp", "expert"), None)
    experts = P("expert", "dp", None)
    in_specs = (tokens, P(), P(), P(), tokens, tokens, experts, experts, experts, tokens)
    return jax.shard_map(
        shards, mesh=mesh, in_specs=in_specs, out_specs=(tokens, tokens), check_vma=False
    )
```

time: 177 us -> 166 us (0.938)
  Pallas kernels: 31.3 us -> 18 us
  local copies, waits for them, and re-layouts: 0 us -> 9.64 us
  waiting for transfers between devices: 31.9 us -> 26.9 us
    pallas_call x2 -> x4, Pallas kernels: 25.8 us -> 15.1 us  [the longest x1 10.8 us: shards(): pl.pallas_call(expert_kernel, out_shape=shape((sources, CHUNK, width), BF...]
    unnamed x0 -> x34, local copies, waits for them, and re-layouts: none -> 9.64 us
    all_gather x1, waiting for transfers between devices: 31.9 us -> 26.9 us  [shards(): weights = lax.all_gather(stacked, 'dp', axis=0, tiled=False)]
    pallas_call x1, Pallas kernels: 5.45 us -> 2.92 us  [shards(): pl.pallas_call(combine_kernel, out_shape=(shape((toks, width), BF), shape...]
  transfers between devices with their start and end apart: 1 -> 1, of which waited for: 1 -> 1; matrix products, arithmetic and copies ran while one was open for 0% -> 0% of each run, Pallas kernels for 3% -> 2%
where the time goes in v2:
time: 166 us; the launch traced here: 165 us
  blocking collectives  96.6 us (58%)
  waiting for transfers between devices  26.9 us (16%)
  Pallas kernels  18 us (11%)
  between operations  14.1 us (8%)
  local copies, waits for them, and re-layouts  9.64 us (6%)
    all_to_all x1, blocking collectives, shards(): lax.all_to_all(send, 'expert', split_axis=0, concat_axis=0, tiled=True)  48.4 us
    all_to_all x1, blocking collectives, shards(): lax.all_to_all(results, 'expert', split_axis=0, concat_axis=0, tiled=True)  48.2 us
    all_gather x1, waiting for transfers between devices, shards(): weights = lax.all_gather(stacked, 'dp', axis=0, tiled=False)  26.9 us
    pallas_call x1, Pallas kernels, shards(): pl.pallas_call(expert_kernel, out_shape=shape((sources, CHUNK, width), BF...  10.8 us
    unnamed x34, local copies, waits for them, and re-layouts  9.64 us
  transfers between devices with their start and end apart: 1, of which 1 were waited for; matrix products, arithmetic and copies ran while one was open for 0% of the time, Pallas kernels for 2%

profile of v2, /device:TPU:1, one launch (start us, length us, event | category | flops | bytes accessed | tf_op | source)
XLA Modules:
  0.0 165.4 jit_solution(9342187101008464083)
XLA Ops:
  7.2 0.0 all-gather.3.cloned.1.call-start
  7.2 0.0 copy-start.7
  7.2 0.9 copy-done.7
  8.1 0.9 copy-done.8
  9.0 0.9 copy-done.9
  9.9 0.7 stack.1
  10.6 0.0 all-gather.3.cloned.1.call-update
  10.7 0.0 copy-start
  10.7 1.7 %copy-done = bf16[1152,1024]{1,0:T(8,128)(2,1)S(1)} copy-done((bf16[1152,1024]{1,0:T(8,128)(2,1)S(1)}, bf16[1152,1024]{1,0:T(8,128)(2,1)}, u32[]{:S(2)}) %copy-start) | copy-done | bytes 2359320
  12.3 0.9 copy-done.2
  13.3 1.0 copy-done.6
  14.2 0.7 copy-done.12
  14.9 0.7 copy-done.14
  15.6 0.7 copy-done.15
  16.3 0.7 copy-done.16
  17.0 3.3 %prepare.1 = (bf16[16,104,1024]{2,1,0:T(8,128)(2,1)S(1)}, bf16[128,1024]{1,0:T(8,128)(2,1)S(1)}, f32[128,1]{1,0:T(8,128)S(1)}, bf16[256,1664]{1,0:T(8,128)(2,1)S(1)}) custom-call(bf16[128,1152]{1,0:T(8,128)(2,1)S(1)} %copy-done.6, bf16[1152,1024]{1,0:T(8,128)(2,1)S(1)} %copy-done, f32[1,1024]{1,0:T(1,128)S(1)} %bitcast.7, f32[1,1024]{1,0:T(1,128)S(1)} %bitcast.5, ...), custom_call_target="tpu_custom_call" | custom-call | tf_op jit(solution)/shard_map/prepare/pallas_call | solution.py:186
  20.3 0.0 copy-start.10
  20.3 0.6 copy-done.10
  20.9 48.4 %all_to_all.10.received = bf16[16,104,1024]{2,1,0:T(8,128)(2,1)S(1)} all-to-all(bf16[16,104,1024]{2,1,0:T(8,128)(2,1)S(1)} %get-tuple-element.6), channel_id=1, replica_groups=mesh['dp'=32,'expert'=16] {'expert'}, dimensions={0} | all-to-all | bytes 6815744 | tf_op jit(solution)/shard_map/all_to_all | solution.py:199
  69.3 0.0 copy-done.4
  69.3 0.3 arrange.1.rows
  69.6 26.9 %all-gather.3.cloned.1.call-done = bf16[192,32,768]{2,1,0:T(8,128)(2,1)} async-done(((bf16[6,32,768]{2,1,0:T(8,128)(2,1)}), bf16[192,32,768]{2,1,0:T(8,128)(2,1)}) %all-gather.3.cloned.1.call-update) | async-done | bytes 9437200 | tf_op jit(solution)/shard_map/all_gather | solution.py:184
  96.5 10.8 %experts.1 = bf16[16,104,1024]{2,1,0:T(8,128)(2,1)S(1)} custom-call(bf16[4,400,1024]{2,1,0:T(8,128)(2,1)S(1)} %arrange.1.rows, bf16[32,6,32,768]{3,2,1,0:T(8,128)(2,1)} %bitcast.10), custom_call_target="tpu_custom_call" | custom-call | tf_op jit(solution)/shard_map/experts/pallas_call | solution.py:209
  107.3 0.0 copy-start.1
  107.3 0.0 copy-start.3
  107.3 0.0 copy-start.11
  107.3 0.0 copy-start.13
  107.3 48.2 %all_to_all.11.back = bf16[16,104,1024]{2,1,0:T(8,128)(2,1)S(1)} all-to-all(bf16[16,104,1024]{2,1,0:T(8,128)(2,1)S(1)} %experts.1), channel_id=1, replica_groups=mesh['dp'=32,'expert'=16] {'expert'}, dimensions={0} | all-to-all | bytes 6815744 | tf_op jit(solution)/shard_map/all_to_all | solution.py:224
  155.6 0.0 copy-done.5
  155.6 0.0 copy-done.11
  155.6 0.0 copy-done.13
  155.6 2.9 %combine.1 = (bf16[128,1024]{1,0:T(8,128)(2,1)}, bf16[128,1152]{1,0:T(8,128)(2,1)}) custom-call(bf16[16,104,1024]{2,1,0:T(8,128)(2,1)S(1)} %all_to_all.11.back, bf16[256,1664]{1,0:T(8,128)(2,1)S(1)} %copy-done.5, bf16[128,1024]{1,0:T(8,128)(2,1)S(1)} %get-tuple-element.8.hidden, f32[128,1]{1,0:T(8,128)S(1)} %copy-done.11, f32[1,1024]{1,0:T(1,128)S(1)} %bitcast.6, ...), custom_call_target="tpu_custom_call" | custom-call | tf_op jit(solution)/shard_map/combine/pallas_call | solution.py:225
  (12 shorter events, 0.0 us)
Async XLA Ops:
  7.2 89.3 %all-gather.3.cloned.1.call-start = ((), (), s32[]{:S(2)}) async-start(), calls=%async_computation.2 | async-start | bytes 9732096 | tf_op jit(solution)/shard_map/all_gather | solution.py:184
  7.2 0.9 copy-start.7
  8.1 0.9 copy-start.8
  9.0 0.9 copy-start.9
  10.7 1.7 %copy-start = (bf16[1152,1024]{1,0:T(8,128)(2,1)S(1)}, bf16[1152,1024]{1,0:T(8,128)(2,1)}, u32[]{:S(2)}) copy-start(bf16[1152,1024]{1,0:T(8,128)(2,1)} %proj.3) | copy-start | bytes 7077892
  12.3 0.9 copy-start.2
  13.3 1.0 copy-start.6
  14.2 0.7 copy-start.12
  14.9 0.7 copy-start.14
  15.6 0.7 copy-start.15
  16.3 0.7 copy-start.16
  20.3 0.6 copy-start.10
  20.9 48.4 %copy-start.4 = (bf16[256,1664]{1,0:T(8,128)(2,1)}, bf16[256,1664]{1,0:T(8,128)(2,1)S(1)}, u32[]{:S(2)}) copy-start(bf16[256,1664]{1,0:T(8,128)(2,1)S(1)} %get-tuple-element.7.mix) | copy-start | bytes 2555908
  107.3 48.3 %copy-start.1 = (bf16[1152,1024]{1,0:T(8,128)(2,1)S(1)}, bf16[1152,1024]{1,0:T(8,128)(2,1)}, u32[]{:S(2)}) copy-start(bf16[1152,1024]{1,0:T(8,128)(2,1)} %proj.3) | copy-start | bytes 7077892
  107.3 48.3 %copy-start.3 = (bf16[128,1024]{1,0:T(8,128)(2,1)S(1)}, bf16[128,1024]{1,0:T(8,128)(2,1)}, u32[]{:S(2)}) copy-start(bf16[128,1024]{1,0:T(8,128)(2,1)} %grads.3) | copy-start | bytes 786436
  107.3 48.3 %copy-start.5 = (bf16[256,1664]{1,0:T(8,128)(2,1)S(1)}, bf16[256,1664]{1,0:T(8,128)(2,1)}, u32[]{:S(2)}) copy-start(bf16[256,1664]{1,0:T(8,128)(2,1)} %copy-done.4) | copy-start | bytes 2555908
  107.3 48.3 %copy-start.11 = (f32[128,1]{1,0:T(8,128)S(1)}, f32[128,1]{1,0:T(8,128)}, u32[]{:S(2)}) copy-start(f32[128,1]{1,0:T(8,128)} %copy-done.10) | copy-start | bytes 1540
  107.3 48.3 %copy-start.13 = (f32[1024]{0:T(1024)S(1)}, f32[1024]{0:T(1024)}, u32[]{:S(2)}) copy-start(f32[1024]{0:T(1024)} %param.13) | copy-start | bytes 12292
Sparse Core Ops, SparseCore 0:
  10.8 85.6 all-gather.2

commit v3 on v2

--- a/solution.py
+++ b/solution.py
@@ -23,7 +23,9 @@
     return lax.dot_general(a, b, (((1,), (1,)), ((), ())), preferred_element_type=F32)
 
 
-def prepare_kernel(feats, proj, bias, gain, ids, codes, grads, send, hidden, inv, mix):
+def prepare_kernel(
+    feats, proj, bias, gain, ids, codes, grads, send, hidden, inv, mix, mix_last
+):
     sources, _, width = send.shape
     rows = sources * CHUNK
     toks = grads.shape[0]
@@ -52,8 +54,16 @@
     of_token = jnp.where(kind < 2, chosen, 0.0)
     of_grad = jnp.where(kind < 2, 0.0, chosen)
     spread = mm(pick, weight.astype(BF))
-    mix[0:toks, :] = (spread * of_token).T.astype(BF)
-    mix[toks : 2 * toks, :] = (spread * of_grad).T.astype(BF)
+    spread = (spread * chosen).reshape(sources, CHUNK, toks)
+    side = LAST // 2
+    for i in range(2):
+        part = spread[:, side * i : side * (i + 1), :]
+        mix[i] = part.reshape(sources * side, toks).T.astype(BF)
+    part = spread[:, LAST:CHUNK, :]
+    row = lax.broadcasted_iota(jnp.int32, (1, CHUNK - LAST, 1), 1)
+    for i in range(2):
+        mine = jnp.where((row < 2) == (i == 0), part, 0.0)
+        mix_last[i] = mine.reshape(sources * (CHUNK - LAST), toks).T.astype(BF)
     from_grads = mm(of_grad.astype(BF), grads[...])
     h = (mm(feats[...], proj[...]) + bias[...]).astype(BF)
     hidden[...] = h
@@ -140,13 +150,20 @@
         c.wait()
 
 
-def combine_kernel(back, mix, hidden, inv, gain, grads, proj, out, feat_grad):
+def combine_kernel(
+    back, mix, mix_last, hidden, inv, gain, grads, proj, out, feat_grad
+):
     n, _, width = back.shape
-    toks = hidden.shape[0]
+    side = LAST // 2
+    last = back[:, LAST:CHUNK, :].reshape(n * (CHUNK - LAST), width)
+
+    def total_of(i):
+        main = back[:, side * i : side * (i + 1), :].reshape(n * side, width)
+        return mm(mix[i], main) + mm(mix_last[i], last)
+
     hf = hidden[...].astype(F32)
-    sums = mm(mix[...], back[...].reshape(n * CHUNK, width))
-    out[...] = (hf + sums[0:toks]).astype(BF)
-    scaled = sums[toks : 2 * toks] * gain[...]
+    out[...] = (hf + total_of(0)).astype(BF)
+    scaled = total_of(1) * gain[...]
     scale = inv[...]
     centre = jnp.mean(hf * scaled, axis=1, keepdims=True)
     total = grads[...].astype(F32) + scale * scaled - hf * (scale * scale * scale) * centre
@@ -178,21 +195,22 @@
         in_specs=[HBM] * 3,
         out_specs=HBM,
         scratch_shapes=[pltpu.SemaphoreType.DMA((3,))],
-        compiler_params=params(16),
+        compiler_params=params(60),
         name="stack",
     )(w_gate, w_up, w_down_t)
     weights = lax.all_gather(stacked, "dp", axis=0, tiled=False)
 
-    send, hidden, inv, mix = pl.pallas_call(
+    send, hidden, inv, mix, mix_last = pl.pallas_call(
         prepare_kernel,
         out_shape=(
             shape((sources, CHUNK, width), BF),
             shape((toks, width), BF),
             shape((toks, 1), F32),
-            shape((2 * toks, sources * CHUNK), BF),
+            shape((2, toks, sources * LAST // 2), BF),
+            shape((2, toks, sources * (CHUNK - LAST)), BF),
         ),
         in_specs=[VMEM] * 7,
-        out_specs=(VMEM,) * 4,
+        out_specs=(VMEM,) * 5,
         compiler_params=params(28),
         name="prepare",
     )(feats, proj, bias, gain, expert_ids.T, gate_codes.T, out_grad)
@@ -225,11 +243,11 @@
     return pl.pallas_call(
         combine_kernel,
         out_shape=(shape((toks, width), BF), shape(feats.shape, BF)),
-        in_specs=[VMEM] * 7,
+        in_specs=[VMEM] * 8,
         out_specs=(VMEM,) * 2,
         compiler_params=params(28),
         name="combine",
-    )(back, mix, hidden, inv, gain, out_grad, proj)
+    )(back, mix, mix_last, hidden, inv, gain, out_grad, proj)
 
 
 def solution(mesh):

time: 166 us -> 172 us (1.036)
  Pallas kernels: 18 us -> 26.7 us
  local copies, waits for them, and re-layouts: 9.64 us -> 6.97 us
    pallas_call x1, Pallas kernels: 0.73 us -> 10.1 us  [shards(): pl.pallas_call(stack_kernel, out_shape=shape((3 * local, part, ff), BF),...]
    unnamed x34 -> x32, local copies, waits for them, and re-layouts: 9.64 us -> 6.97 us
where the time goes in v3:
time: 172 us
  blocking collectives  97 us (56%)
  waiting for transfers between devices  26.8 us (16%)
  Pallas kernels  26.7 us (16%)
  between operations  14.2 us (8%)
  local copies, waits for them, and re-layouts  6.97 us (4%)
    all_to_all x1, blocking collectives, shards(): lax.all_to_all(results, 'expert', split_axis=0, concat_axis=0, tiled=True)  48.6 us
    all_to_all x1, blocking collectives, shards(): lax.all_to_all(send, 'expert', split_axis=0, concat_axis=0, tiled=True)  48.4 us
    all_gather x1, waiting for transfers between devices, shards(): weights = lax.all_gather(stacked, 'dp', axis=0, tiled=False)  26.8 us
    pallas_call x1, Pallas kernels, shards(): pl.pallas_call(expert_kernel, out_shape=shape((sources, CHUNK, width), BF...  10.8 us
    pallas_call x1, Pallas kernels, shards(): pl.pallas_call(stack_kernel, out_shape=shape((3 * local, part, ff), BF),...  10.1 us
    unnamed x32, local copies, waits for them, and re-layouts  6.97 us
  transfers between devices with their start and end apart: 1, of which 1 were waited for; matrix products, arithmetic and copies ran while one was open for 0% of the time, Pallas kernels for 2%

profile of v3, /device:TPU:1, one launch (start us, length us, event | category | flops | bytes accessed | tf_op | source)
XLA Modules:
  0.0 171.6 jit_solution(8999518413486749697)
XLA Ops:
  7.2 0.0 all-gather.3.cloned.1.call-start
  7.2 10.1 %stack.1 = bf16[6,32,768]{2,1,0:T(8,128)(2,1)} custom-call(bf16[2,32,768]{2,1,0:T(8,128)(2,1)} %w_gate.1, bf16[2,32,768]{2,1,0:T(8,128)(2,1)} %w_up.1, bf16[2,32,768]{2,1,0:T(8,128)(2,1)} %w_down_t.1), custom_call_target="tpu_custom_call" | custom-call | tf_op jit(solution)/shard_map/stack/pallas_call | solution.py:192
  17.3 0.0 all-gather.3.cloned.1.call-update
  17.3 0.0 copy-start
  17.3 1.7 copy-done
  19.0 0.9 copy-done.2
  19.9 1.0 copy-done.6
  20.9 0.7 copy-done.11
  21.6 0.7 copy-done.13
  22.3 0.7 copy-done.14
  23.0 0.7 copy-done.15
  23.6 3.2 %prepare.1 = (bf16[16,104,1024]{2,1,0:T(8,128)(2,1)S(1)}, bf16[128,1024]{1,0:T(8,128)(2,1)S(1)}, f32[128,1]{1,0:T(8,128)S(1)}, bf16[2,128,768]{2,1,0:T(8,128)(2,1)S(1)}, bf16[2,128,128]{2,1,0:T(8,128)(2,1)S(1)}) custom-call(bf16[128,1152]{1,0:T(8,128)(2,1)S(1)} %copy-done.6, bf16[1152,1024]{1,0:T(8,128)(2,1)S(1)} %copy-done, f32[1,1024]{1,0:T(1,128)S(1)} %bitcast.7, ...), custom_call_target="tpu_custom_call" | custom-call | tf_op jit(solution)/shard_map/prepare/pallas_call | solution.py:203
  26.8 0.0 copy-start.7
  26.8 0.6 copy-done.7
  27.4 48.4 %all_to_all.10.received = bf16[16,104,1024]{2,1,0:T(8,128)(2,1)S(1)} all-to-all(bf16[16,104,1024]{2,1,0:T(8,128)(2,1)S(1)} %get-tuple-element.7), channel_id=1, replica_groups=mesh['dp'=32,'expert'=16] {'expert'}, dimensions={0} | all-to-all | bytes 6815744 | tf_op jit(solution)/shard_map/all_to_all | solution.py:217
  75.8 0.0 copy-done.4
  75.8 0.0 copy-done.9
  75.8 0.3 arrange.1.rows
  76.1 26.8 %all-gather.3.cloned.1.call-done = bf16[192,32,768]{2,1,0:T(8,128)(2,1)} async-done(((bf16[6,32,768]{2,1,0:T(8,128)(2,1)}), bf16[192,32,768]{2,1,0:T(8,128)(2,1)}) %all-gather.3.cloned.1.call-update) | async-done | bytes 9437200 | tf_op jit(solution)/shard_map/all_gather | solution.py:201
  102.9 10.8 %experts.1 = bf16[16,104,1024]{2,1,0:T(8,128)(2,1)S(1)} custom-call(bf16[4,400,1024]{2,1,0:T(8,128)(2,1)S(1)} %arrange.1.rows, bf16[32,6,32,768]{3,2,1,0:T(8,128)(2,1)} %bitcast.10), custom_call_target="tpu_custom_call" | custom-call | tf_op jit(solution)/shard_map/experts/pallas_call | solution.py:227
  113.7 0.0 copy-start.1
  113.7 0.0 copy-start.3
  113.7 0.0 copy-start.5
  113.7 0.0 copy-start.8
  113.7 0.0 copy-start.10
  113.7 0.0 copy-start.12
  113.7 48.6 %all_to_all.11.back = bf16[16,104,1024]{2,1,0:T(8,128)(2,1)S(1)} all-to-all(bf16[16,104,1024]{2,1,0:T(8,128)(2,1)S(1)} %experts.1), channel_id=1, replica_groups=mesh['dp'=32,'expert'=16] {'expert'}, dimensions={0} | all-to-all | bytes 6815744 | tf_op jit(solution)/shard_map/all_to_all | solution.py:242
  162.4 0.0 copy-done.1
  162.4 0.0 copy-done.3
  162.4 0.0 copy-done.5
  162.4 0.0 copy-done.8
  162.4 2.4 %combine.1 = (bf16[128,1024]{1,0:T(8,128)(2,1)}, bf16[128,1152]{1,0:T(8,128)(2,1)}) custom-call(bf16[16,104,1024]{2,1,0:T(8,128)(2,1)S(1)} %all_to_all.11.back, bf16[2,128,768]{2,1,0:T(8,128)(2,1)S(1)} %copy-done.5, bf16[2,128,128]{2,1,0:T(8,128)(2,1)S(1)} %copy-done.10, bf16[128,1024]{1,0:T(8,128)(2,1)S(1)} %get-tuple-element.10.hidden, ...), custom_call_target="tpu_custom_call" | custom-call | tf_op jit(solution)/shard_map/combine/pallas_call | solution.py:243
  (10 shorter events, 0.0 us)
Async XLA Ops:
  7.2 95.7 %all-gather.3.cloned.1.call-start = ((), (), s32[]{:S(2)}) async-start(), calls=%async_computation.2 | async-start | bytes 9732096 | tf_op jit(solution)/shard_map/all_gather | solution.py:201
  17.3 1.7 copy-start
  19.0 0.9 copy-start.2
  19.9 1.0 copy-start.6
  20.9 0.7 copy-start.11
  21.6 0.7 copy-start.13
  22.3 0.7 copy-start.14
  22.9 0.7 copy-start.15
  26.8 0.6 copy-start.7
  27.4 48.4 %copy-start.4 = (bf16[2,128,768]{2,1,0:T(8,128)(2,1)}, bf16[2,128,768]{2,1,0:T(8,128)(2,1)S(1)}, u32[]{:S(2)}) copy-start(bf16[2,128,768]{2,1,0:T(8,128)(2,1)S(1)} %get-tuple-element.8.mix) | copy-start | bytes 1179652
  27.4 48.4 %copy-start.9 = (bf16[2,128,128]{2,1,0:T(8,128)(2,1)}, bf16[2,128,128]{2,1,0:T(8,128)(2,1)S(1)}, u32[]{:S(2)}) copy-start(bf16[2,128,128]{2,1,0:T(8,128)(2,1)S(1)} %get-tuple-element.9.mix_last) | copy-start | bytes 196612
  113.7 48.7 %copy-start.1 = (bf16[1152,1024]{1,0:T(8,128)(2,1)S(1)}, bf16[1152,1024]{1,0:T(8,128)(2,1)}, u32[]{:S(2)}) copy-start(bf16[1152,1024]{1,0:T(8,128)(2,1)} %proj.3) | copy-start | bytes 7077892
  113.7 48.7 %copy-start.3 = (bf16[128,1024]{1,0:T(8,128)(2,1)S(1)}, bf16[128,1024]{1,0:T(8,128)(2,1)}, u32[]{:S(2)}) copy-start(bf16[128,1024]{1,0:T(8,128)(2,1)} %grads.3) | copy-start | bytes 786436
  113.7 48.7 %copy-start.5 = (bf16[2,128,768]{2,1,0:T(8,128)(2,1)S(1)}, bf16[2,128,768]{2,1,0:T(8,128)(2,1)}, u32[]{:S(2)}) copy-start(bf16[2,128,768]{2,1,0:T(8,128)(2,1)} %copy-done.4) | copy-start | bytes 1179652
  113.7 48.7 %copy-start.8 = (f32[128,1]{1,0:T(8,128)S(1)}, f32[128,1]{1,0:T(8,128)}, u32[]{:S(2)}) copy-start(f32[128,1]{1,0:T(8,128)} %copy-done.7) | copy-start | bytes 1540
  113.7 48.7 %copy-start.10 = (bf16[2,128,128]{2,1,0:T(8,128)(2,1)S(1)}, bf16[2,128,128]{2,1,0:T(8,128)(2,1)}, u32[]{:S(2)}) copy-start(bf16[2,128,128]{2,1,0:T(8,128)(2,1)} %copy-done.9) | copy-start | bytes 196612
  113.7 48.7 %copy-start.12 = (f32[1024]{0:T(1024)S(1)}, f32[1024]{0:T(1024)}, u32[]{:S(2)}) copy-start(f32[1024]{0:T(1024)} %param.13) | copy-start | bytes 12292
Sparse Core Ops, SparseCore 0:
  17.4 85.4 all-gather.2

commit v4 on v3

--- a/solution.py
+++ b/solution.py
@@ -195,7 +195,7 @@
         in_specs=[HBM] * 3,
         out_specs=HBM,
         scratch_shapes=[pltpu.SemaphoreType.DMA((3,))],
-        compiler_params=params(60),
+        compiler_params=params(16),
         name="stack",
     )(w_gate, w_up, w_down_t)
     weights = lax.all_gather(stacked, "dp", axis=0, tiled=False)

time: 172 us -> 165 us (0.959)
  Pallas kernels: 26.7 us -> 17.3 us
  local copies, waits for them, and re-layouts: 6.97 us -> 9.65 us
    pallas_call x1, Pallas kernels: 10.1 us -> 0.73 us  [shards(): pl.pallas_call(stack_kernel, out_shape=shape((3 * local, part, ff), BF),...]
    unnamed x32 -> x38, local copies, waits for them, and re-layouts: 6.97 us -> 9.65 us
where the time goes in v4:
time: 165 us
  blocking collectives  96.8 us (59%)
  waiting for transfers between devices  27 us (16%)
  Pallas kernels  17.3 us (10%)
  between operations  14.2 us (9%)
  local copies, waits for them, and re-layouts  9.65 us (6%)
    all_to_all x1, blocking collectives, shards(): lax.all_to_all(results, 'expert', split_axis=0, concat_axis=0, tiled=True)  48.4 us
    all_to_all x1, blocking collectives, shards(): lax.all_to_all(send, 'expert', split_axis=0, concat_axis=0, tiled=True)  48.4 us
    all_gather x1, waiting for transfers between devices, shards(): weights = lax.all_gather(stacked, 'dp', axis=0, tiled=False)  27 us
    pallas_call x1, Pallas kernels, shards(): pl.pallas_call(expert_kernel, out_shape=shape((sources, CHUNK, width), BF...  10.8 us
    unnamed x38, local copies, waits for them, and re-layouts  9.65 us
  transfers between devices with their start and end apart: 1, of which 1 were waited for; matrix products, arithmetic and copies ran while one was open for 0% of the time, Pallas kernels for 2%

profile of v4, /device:TPU:1, one launch (start us, length us, event | category | flops | bytes accessed | tf_op | source)
XLA Modules:
  0.0 165.0 jit_solution(15981872410833881318)
XLA Ops:
  7.2 0.0 all-gather.3.cloned.1.call-start
  7.2 0.0 copy-start.7
  7.2 0.9 copy-done.7
  8.1 0.9 copy-done.8
  9.0 0.9 copy-done.9
  9.9 0.7 stack.1
  10.6 0.0 all-gather.3.cloned.1.call-update
  10.7 0.0 copy-start
  10.7 1.7 %copy-done = bf16[1152,1024]{1,0:T(8,128)(2,1)S(1)} copy-done((bf16[1152,1024]{1,0:T(8,128)(2,1)S(1)}, bf16[1152,1024]{1,0:T(8,128)(2,1)}, u32[]{:S(2)}) %copy-start) | copy-done | bytes 2359320
  12.3 0.9 copy-done.2
  13.3 1.0 copy-done.6
  14.2 0.7 copy-done.14
  14.9 0.7 copy-done.16
  15.6 0.7 copy-done.17
  16.3 0.7 copy-done.18
  17.0 3.2 %prepare.1 = (bf16[16,104,1024]{2,1,0:T(8,128)(2,1)S(1)}, bf16[128,1024]{1,0:T(8,128)(2,1)S(1)}, f32[128,1]{1,0:T(8,128)S(1)}, bf16[2,128,768]{2,1,0:T(8,128)(2,1)S(1)}, bf16[2,128,128]{2,1,0:T(8,128)(2,1)S(1)}) custom-call(bf16[128,1152]{1,0:T(8,128)(2,1)S(1)} %copy-done.6, bf16[1152,1024]{1,0:T(8,128)(2,1)S(1)} %copy-done, f32[1,1024]{1,0:T(1,128)S(1)} %bitcast.7, ...), custom_call_target="tpu_custom_call" | custom-call | tf_op jit(solution)/shard_map/prepare/pallas_call | solution.py:203
  20.2 0.0 copy-start.10
  20.2 0.6 copy-done.10
  20.8 48.4 %all_to_all.10.received = bf16[16,104,1024]{2,1,0:T(8,128)(2,1)S(1)} all-to-all(bf16[16,104,1024]{2,1,0:T(8,128)(2,1)S(1)} %get-tuple-element.7), channel_id=1, replica_groups=mesh['dp'=32,'expert'=16] {'expert'}, dimensions={0} | all-to-all | bytes 6815744 | tf_op jit(solution)/shard_map/all_to_all | solution.py:217
  69.2 0.0 copy-done.12
  69.2 0.3 arrange.1.rows
  69.5 27.0 %all-gather.3.cloned.1.call-done = bf16[192,32,768]{2,1,0:T(8,128)(2,1)} async-done(((bf16[6,32,768]{2,1,0:T(8,128)(2,1)}), bf16[192,32,768]{2,1,0:T(8,128)(2,1)}) %all-gather.3.cloned.1.call-update) | async-done | bytes 9437200 | tf_op jit(solution)/shard_map/all_gather | solution.py:201
  96.5 10.8 %experts.1 = bf16[16,104,1024]{2,1,0:T(8,128)(2,1)S(1)} custom-call(bf16[4,400,1024]{2,1,0:T(8,128)(2,1)S(1)} %arrange.1.rows, bf16[32,6,32,768]{3,2,1,0:T(8,128)(2,1)} %bitcast.10), custom_call_target="tpu_custom_call" | custom-call | tf_op jit(solution)/shard_map/experts/pallas_call | solution.py:227
  107.3 0.0 copy-start.1
  107.3 0.0 copy-start.3
  107.3 0.0 copy-start.13
  107.3 0.0 copy-start.15
  107.4 48.4 %all_to_all.11.back = bf16[16,104,1024]{2,1,0:T(8,128)(2,1)S(1)} all-to-all(bf16[16,104,1024]{2,1,0:T(8,128)(2,1)S(1)} %experts.1), channel_id=1, replica_groups=mesh['dp'=32,'expert'=16] {'expert'}, dimensions={0} | all-to-all | bytes 6815744 | tf_op jit(solution)/shard_map/all_to_all | solution.py:242
  155.8 0.0 copy-done.11
  155.8 0.0 copy-done.13
  155.8 0.0 copy-done.15
  155.8 2.4 %combine.1 = (bf16[128,1024]{1,0:T(8,128)(2,1)}, bf16[128,1152]{1,0:T(8,128)(2,1)}) custom-call(bf16[16,104,1024]{2,1,0:T(8,128)(2,1)S(1)} %all_to_all.11.back, bf16[2,128,768]{2,1,0:T(8,128)(2,1)S(1)} %copy-done.5, bf16[2,128,128]{2,1,0:T(8,128)(2,1)S(1)} %copy-done.13, bf16[128,1024]{1,0:T(8,128)(2,1)S(1)} %get-tuple-element.10.hidden, ...), custom_call_target="tpu_custom_call" | custom-call | tf_op jit(solution)/shard_map/combine/pallas_call | solution.py:243
  (16 shorter events, 0.0 us)
Async XLA Ops:
  7.2 89.3 %all-gather.3.cloned.1.call-start = ((), (), s32[]{:S(2)}) async-start(), calls=%async_computation.2 | async-start | bytes 9732096 | tf_op jit(solution)/shard_map/all_gather | solution.py:201
  7.2 0.9 copy-start.7
  8.1 0.9 copy-start.8
  9.0 0.9 copy-start.9
  10.7 1.7 %copy-start = (bf16[1152,1024]{1,0:T(8,128)(2,1)S(1)}, bf16[1152,1024]{1,0:T(8,128)(2,1)}, u32[]{:S(2)}) copy-start(bf16[1152,1024]{1,0:T(8,128)(2,1)} %proj.3) | copy-start | bytes 7077892
  12.3 0.9 copy-start.2
  13.3 1.0 copy-start.6
  14.2 0.7 copy-start.14
  14.9 0.7 copy-start.16
  15.6 0.7 copy-start.17
  16.3 0.7 copy-start.18
  20.2 0.6 copy-start.10
  20.8 48.4 %copy-start.4 = (bf16[2,128,768]{2,1,0:T(8,128)(2,1)}, bf16[2,128,768]{2,1,0:T(8,128)(2,1)S(1)}, u32[]{:S(2)}) copy-start(bf16[2,128,768]{2,1,0:T(8,128)(2,1)S(1)} %get-tuple-element.8.mix) | copy-start | bytes 1179652
  20.8 48.4 %copy-start.12 = (bf16[2,128,128]{2,1,0:T(8,128)(2,1)}, bf16[2,128,128]{2,1,0:T(8,128)(2,1)S(1)}, u32[]{:S(2)}) copy-start(bf16[2,128,128]{2,1,0:T(8,128)(2,1)S(1)} %get-tuple-element.9.mix_last) | copy-start | bytes 196612
  107.3 48.5 %copy-start.1 = (bf16[1152,1024]{1,0:T(8,128)(2,1)S(1)}, bf16[1152,1024]{1,0:T(8,128)(2,1)}, u32[]{:S(2)}) copy-start(bf16[1152,1024]{1,0:T(8,128)(2,1)} %proj.3) | copy-start | bytes 7077892
  107.3 48.5 %copy-start.3 = (bf16[128,1024]{1,0:T(8,128)(2,1)S(1)}, bf16[128,1024]{1,0:T(8,128)(2,1)}, u32[]{:S(2)}) copy-start(bf16[128,1024]{1,0:T(8,128)(2,1)} %grads.3) | copy-start | bytes 786436
  107.3 48.5 %copy-start.5 = (bf16[2,128,768]{2,1,0:T(8,128)(2,1)S(1)}, bf16[2,128,768]{2,1,0:T(8,128)(2,1)}, u32[]{:S(2)}) copy-start(bf16[2,128,768]{2,1,0:T(8,128)(2,1)} %copy-done.4) | copy-start | bytes 1179652
  107.3 48.5 %copy-start.11 = (f32[128,1]{1,0:T(8,128)S(1)}, f32[128,1]{1,0:T(8,128)}, u32[]{:S(2)}) copy-start(f32[128,1]{1,0:T(8,128)} %copy-done.10) | copy-start | bytes 1540
  107.3 48.5 %copy-start.13 = (bf16[2,128,128]{2,1,0:T(8,128)(2,1)S(1)}, bf16[2,128,128]{2,1,0:T(8,128)(2,1)}, u32[]{:S(2)}) copy-start(bf16[2,128,128]{2,1,0:T(8,128)(2,1)} %copy-done.12) | copy-start | bytes 196612
  107.3 48.5 %copy-start.15 = (f32[1024]{0:T(1024)S(1)}, f32[1024]{0:T(1024)}, u32[]{:S(2)}) copy-start(f32[1024]{0:T(1024)} %param.13) | copy-start | bytes 12292
Sparse Core Ops, SparseCore 0:
  10.8 85.6 all-gather.2

commit v5 on v4

--- a/solution.py
+++ b/solution.py
@@ -84,53 +84,48 @@
         rows[k, sources * MAIN :, :] = last[:, k, :].astype(BF)
 
 
-def expert_kernel(rows, weights, back, buf, mixed, d_gate, d_up, sems):
+def expert_kernel(rows, weights, back, wide, down, mixed, d_wide, sems):
     sources, _, width = back.shape
     total = rows.shape[1]
-    shards_of, part, ff = buf.shape[1:]
+    shards_of, part, ff = down.shape[1:]
     half = total // 32 * 16
     blocks = (slice(0, half), slice(half, total))
-    copies = {
-        j: pltpu.make_async_copy(weights.at[:, j], buf.at[j], sems.at[j])
-        for j in (0, 2, 4, 1, 3, 5)
-    }
-    for c in copies.values():
-        c.start()
-    ready, last = set(), {}
-
-    def matrix(j):
-        if j not in ready:
-            copies[j].wait()
-            ready.add(j)
-        return buf[j].reshape(shards_of * part, ff)
+    copies = {}
+    for e in range(2):
+        for j, to in (
+            (e, wide.at[e, :, :, 0:ff]),
+            (2 + e, wide.at[e, :, :, ff : 2 * ff]),
+            (4 + e, down.at[e]),
+        ):
+            copies[j] = pltpu.make_async_copy(weights.at[:, j], to, sems.at[j])
+            copies[j].start()
+    last = {}
+
+    def gate_up(e, at):
+        return wide[e, :, :, at].reshape(shards_of * part, at.stop - at.start)
 
     def store(kind, result):
         main = result[0 : sources * MAIN].reshape(sources, MAIN, width)
         back[:, MAIN * kind : MAIN * (kind + 1), :] = main.astype(BF)
         last[kind] = result[sources * MAIN :].reshape(sources, 1, width)
 
-    def first_products(e):
-        h = [mm(rows[e, at, :], matrix(e)) for at in blocks]
-        u = [mm(rows[e, at, :], matrix(2 + e)) for at in blocks]
-        g = [mm(rows[2 + e, at, :], matrix(4 + e)) for at in blocks]
-        return h, u, g
-
-    def elementwise(e, i, h, u, g):
-        sig = jax.nn.sigmoid(h[i])
-        swished = h[i] * sig
-        mixed[e, blocks[i], :] = (swished * u[i]).astype(BF)
-        d_gate[e, blocks[i], :] = (g[i] * (u[i] * (sig * (1.0 + h[i] * (1.0 - sig))))).astype(BF)
-        d_up[e, blocks[i], :] = (g[i] * swished).astype(BF)
-
-    def second_products(e):
-        store(e, mm_t(mixed[e], matrix(4 + e)))
-        store(2 + e, mm_t(d_gate[e], matrix(e)) + mm_t(d_up[e], matrix(2 + e)))
-
     for e in range(2):
-        products = first_products(e)
-        for i in range(2):
-            elementwise(e, i, *products)
-        second_products(e)
+        copies[e].wait()
+        h = [mm(rows[e, at, :], gate_up(e, slice(0, ff))) for at in blocks]
+        copies[2 + e].wait()
+        u = [mm(rows[e, at, :], gate_up(e, slice(ff, 2 * ff))) for at in blocks]
+        copies[4 + e].wait()
+        down_t = down[e].reshape(shards_of * part, ff)
+        g = [mm(rows[2 + e, at, :], down_t) for at in blocks]
+        for i, at in enumerate(blocks):
+            sig = jax.nn.sigmoid(h[i])
+            swished = h[i] * sig
+            mixed[e, at, :] = (swished * u[i]).astype(BF)
+            slope = sig * (1.0 + h[i] * (1.0 - sig))
+            d_wide[e, at, 0:ff] = (g[i] * (u[i] * slope)).astype(BF)
+            d_wide[e, at, ff : 2 * ff] = (g[i] * swished).astype(BF)
+        store(e, mm_t(mixed[e], down_t))
+        store(2 + e, mm_t(d_wide[e], gate_up(e, slice(0, 2 * ff))))
     row = lax.broadcasted_iota(jnp.int32, (1, CHUNK - LAST, 1), 1)
     rest = jnp.zeros((sources, CHUNK - LAST, width), F32)
     for kind in range(KINDS):
@@ -230,10 +225,10 @@
         in_specs=[VMEM, HBM],
         out_specs=VMEM,
         scratch_shapes=[
-            pltpu.VMEM((3 * local, weights.shape[0], part, ff), BF),
+            pltpu.VMEM((local, weights.shape[0], part, 2 * ff), BF),
+            pltpu.VMEM((local, weights.shape[0], part, ff), BF),
             pltpu.VMEM((local, slots, ff), BF),
-            pltpu.VMEM((local, slots, ff), BF),
-            pltpu.VMEM((local, slots, ff), BF),
+            pltpu.VMEM((local, slots, 2 * ff), BF),
             pltpu.SemaphoreType.DMA((3 * local,)),
         ],
         compiler_params=params(46),

time: 165 us -> 165 us (level)
  no operation moved by 1% of the time
where the time goes in v5:
time: 165 us
  blocking collectives  96.8 us (59%)
  waiting for transfers between devices  27 us (16%)
  Pallas kernels  17.2 us (10%)
  between operations  14.2 us (9%)
  local copies, waits for them, and re-layouts  9.65 us (6%)
    all_to_all x1, blocking collectives, shards(): lax.all_to_all(results, 'expert', split_axis=0, concat_axis=0, tiled=True)  48.4 us
    all_to_all x1, blocking collectives, shards(): lax.all_to_all(send, 'expert', split_axis=0, concat_axis=0, tiled=True)  48.4 us
    all_gather x1, waiting for transfers between devices, shards(): weights = lax.all_gather(stacked, 'dp', axis=0, tiled=False)  27 us
    pallas_call x1, Pallas kernels, shards(): pl.pallas_call(expert_kernel, out_shape=shape((sources, CHUNK, width), BF...  10.7 us
    unnamed x38, local copies, waits for them, and re-layouts  9.65 us
  transfers between devices with their start and end apart: 1, of which 1 were waited for; matrix products, arithmetic and copies ran while one was open for 0% of the time, Pallas kernels for 2%

profile of v5, /device:TPU:1, one launch (start us, length us, event | category | flops | bytes accessed | tf_op | source)
XLA Modules:
  0.0 164.9 jit_solution(3065033573337442280)
XLA Ops:
  7.2 0.0 all-gather.3.cloned.1.call-start
  7.2 0.0 copy-start.7
  7.2 0.9 copy-done.7
  8.1 0.9 copy-done.8
  9.0 0.9 copy-done.9
  9.9 0.7 stack.1
  10.6 0.0 all-gather.3.cloned.1.call-update
  10.7 0.0 copy-start
  10.7 1.7 %copy-done = bf16[1152,1024]{1,0:T(8,128)(2,1)S(1)} copy-done((bf16[1152,1024]{1,0:T(8,128)(2,1)S(1)}, bf16[1152,1024]{1,0:T(8,128)(2,1)}, u32[]{:S(2)}) %copy-start) | copy-done | bytes 2359320
  12.3 0.9 copy-done.2
  13.3 1.0 copy-done.6
  14.2 0.7 copy-done.14
  14.9 0.7 copy-done.16
  15.6 0.7 copy-done.17
  16.3 0.7 copy-done.18
  17.0 3.2 %prepare.1 = (bf16[16,104,1024]{2,1,0:T(8,128)(2,1)S(1)}, bf16[128,1024]{1,0:T(8,128)(2,1)S(1)}, f32[128,1]{1,0:T(8,128)S(1)}, bf16[2,128,768]{2,1,0:T(8,128)(2,1)S(1)}, bf16[2,128,128]{2,1,0:T(8,128)(2,1)S(1)}) custom-call(bf16[128,1152]{1,0:T(8,128)(2,1)S(1)} %copy-done.6, bf16[1152,1024]{1,0:T(8,128)(2,1)S(1)} %copy-done, f32[1,1024]{1,0:T(1,128)S(1)} %bitcast.7, ...), custom_call_target="tpu_custom_call" | custom-call | tf_op jit(solution)/shard_map/prepare/pallas_call | solution.py:198
  20.2 0.0 copy-start.10
  20.2 0.6 copy-done.10
  20.8 48.4 %all_to_all.10.received = bf16[16,104,1024]{2,1,0:T(8,128)(2,1)S(1)} all-to-all(bf16[16,104,1024]{2,1,0:T(8,128)(2,1)S(1)} %get-tuple-element.7), channel_id=1, replica_groups=mesh['dp'=32,'expert'=16] {'expert'}, dimensions={0} | all-to-all | bytes 6815744 | tf_op jit(solution)/shard_map/all_to_all | solution.py:212
  69.2 0.3 arrange.1.rows
  69.5 27.0 %all-gather.3.cloned.1.call-done = bf16[192,32,768]{2,1,0:T(8,128)(2,1)} async-done(((bf16[6,32,768]{2,1,0:T(8,128)(2,1)}), bf16[192,32,768]{2,1,0:T(8,128)(2,1)}) %all-gather.3.cloned.1.call-update) | async-done | bytes 9437200 | tf_op jit(solution)/shard_map/all_gather | solution.py:196
  96.5 10.7 %experts.1 = bf16[16,104,1024]{2,1,0:T(8,128)(2,1)S(1)} custom-call(bf16[4,400,1024]{2,1,0:T(8,128)(2,1)S(1)} %arrange.1.rows, bf16[32,6,32,768]{3,2,1,0:T(8,128)(2,1)} %bitcast.10), custom_call_target="tpu_custom_call" | custom-call | tf_op jit(solution)/shard_map/experts/pallas_call | solution.py:222
  107.2 0.0 copy-start.1
  107.2 0.0 copy-start.3
  107.3 0.0 copy-start.13
  107.3 0.0 copy-start.15
  107.3 48.4 %all_to_all.11.back = bf16[16,104,1024]{2,1,0:T(8,128)(2,1)S(1)} all-to-all(bf16[16,104,1024]{2,1,0:T(8,128)(2,1)S(1)} %experts.1), channel_id=1, replica_groups=mesh['dp'=32,'expert'=16] {'expert'}, dimensions={0} | all-to-all | bytes 6815744 | tf_op jit(solution)/shard_map/all_to_all | solution.py:237
  155.7 0.0 copy-done.5
  155.7 0.0 copy-done.11
  155.7 0.0 copy-done.13
  155.7 0.0 copy-done.15
  155.7 2.3 %combine.1 = (bf16[128,1024]{1,0:T(8,128)(2,1)}, bf16[128,1152]{1,0:T(8,128)(2,1)}) custom-call(bf16[16,104,1024]{2,1,0:T(8,128)(2,1)S(1)} %all_to_all.11.back, bf16[2,128,768]{2,1,0:T(8,128)(2,1)S(1)} %copy-done.5, bf16[2,128,128]{2,1,0:T(8,128)(2,1)S(1)} %copy-done.13, bf16[128,1024]{1,0:T(8,128)(2,1)S(1)} %get-tuple-element.10.hidden, ...), custom_call_target="tpu_custom_call" | custom-call | tf_op jit(solution)/shard_map/combine/pallas_call | solution.py:238
  (16 shorter events, 0.0 us)
Async XLA Ops:
  7.2 89.3 %all-gather.3.cloned.1.call-start = ((), (), s32[]{:S(2)}) async-start(), calls=%async_computation.2 | async-start | bytes 9732096 | tf_op jit(solution)/shard_map/all_gather | solution.py:196
  7.2 0.9 copy-start.7
  8.1 0.9 copy-start.8
  9.0 0.9 copy-start.9
  10.7 1.7 %copy-start = (bf16[1152,1024]{1,0:T(8,128)(2,1)S(1)}, bf16[1152,1024]{1,0:T(8,128)(2,1)}, u32[]{:S(2)}) copy-start(bf16[1152,1024]{1,0:T(8,128)(2,1)} %proj.3) | copy-start | bytes 7077892
  12.3 0.9 copy-start.2
  13.3 1.0 copy-start.6
  14.2 0.7 copy-start.14
  14.9 0.7 copy-start.16
  15.6 0.7 copy-start.17
  16.3 0.7 copy-start.18
  20.2 0.6 copy-start.10
  20.8 48.4 %copy-start.4 = (bf16[2,128,768]{2,1,0:T(8,128)(2,1)}, bf16[2,128,768]{2,1,0:T(8,128)(2,1)S(1)}, u32[]{:S(2)}) copy-start(bf16[2,128,768]{2,1,0:T(8,128)(2,1)S(1)} %get-tuple-element.8.mix) | copy-start | bytes 1179652
  20.8 48.4 %copy-start.12 = (bf16[2,128,128]{2,1,0:T(8,128)(2,1)}, bf16[2,128,128]{2,1,0:T(8,128)(2,1)S(1)}, u32[]{:S(2)}) copy-start(bf16[2,128,128]{2,1,0:T(8,128)(2,1)S(1)} %get-tuple-element.9.mix_last) | copy-start | bytes 196612
  107.2 48.5 %copy-start.1 = (bf16[1152,1024]{1,0:T(8,128)(2,1)S(1)}, bf16[1152,1024]{1,0:T(8,128)(2,1)}, u32[]{:S(2)}) copy-start(bf16[1152,1024]{1,0:T(8,128)(2,1)} %proj.3) | copy-start | bytes 7077892
  107.2 48.5 %copy-start.3 = (bf16[128,1024]{1,0:T(8,128)(2,1)S(1)}, bf16[128,1024]{1,0:T(8,128)(2,1)}, u32[]{:S(2)}) copy-start(bf16[128,1024]{1,0:T(8,128)(2,1)} %grads.3) | copy-start | bytes 786436
  107.2 48.5 %copy-start.5 = (bf16[2,128,768]{2,1,0:T(8,128)(2,1)S(1)}, bf16[2,128,768]{2,1,0:T(8,128)(2,1)}, u32[]{:S(2)}) copy-start(bf16[2,128,768]{2,1,0:T(8,128)(2,1)} %copy-done.4) | copy-start | bytes 1179652
  107.2 48.5 %copy-start.11 = (f32[128,1]{1,0:T(8,128)S(1)}, f32[128,1]{1,0:T(8,128)}, u32[]{:S(2)}) copy-start(f32[128,1]{1,0:T(8,128)} %copy-done.10) | copy-start | bytes 1540
  107.3 48.5 %copy-start.13 = (bf16[2,128,128]{2,1,0:T(8,128)(2,1)S(1)}, bf16[2,128,128]{2,1,0:T(8,128)(2,1)}, u32[]{:S(2)}) copy-start(bf16[2,128,128]{2,1,0:T(8,128)(2,1)} %copy-done.12) | copy-start | bytes 196612
  107.3 48.5 %copy-start.15 = (f32[1024]{0:T(1024)S(1)}, f32[1024]{0:T(1024)}, u32[]{:S(2)}) copy-start(f32[1024]{0:T(1024)} %param.13) | copy-start | bytes 12292
Sparse Core Ops, SparseCore 0:
  10.8 85.6 all-gather.2
